TPU v7x, 512 devices: a whole 4x8x8 slice. The times are simulated.
512 devices in a mesh: chan: 16 (over y_lo, x, core), space: 32 (over z, y_hi).
Axes of the slice: x: 4, y: 8 (y_hi: 4, y_lo: 2; y = y_hi * 2 + y_lo), z: 8, core: 2. Of those that a mesh axis runs over, the one named last changes fastest.
Arguments:
- fields: bfloat16 [1, 20, 512, 1024], P(None, None, 'chan', 'space'), may hold values from -6 to 6
- stem_weight: bfloat16 [3, 3, 20, 32], replicated, may hold values from -0.4375 to 0.4375
- stem_bias: float32 [32], replicated, may hold values from -3 to 3
- embed_weight: bfloat16 [7, 7, 32, 1024], P(None, None, None, 'chan'), may hold values from -0.4 to 0.4
- embed_bias: float32 [1024], replicated, may hold values from -3 to 3
- norm_gain: float32 [1024], replicated, may hold values from 0.5 to 1.5
- norm_bias: float32 [1024], replicated, may hold values from -3 to 3
- mix_in: bfloat16 [32768, 1024], P('space', 'chan'), may hold values from -0.03125 to 0.03125
- mix_in_bias: float32 [1024], replicated, may hold values from -3 to 3
- mix_out: bfloat16 [1024, 32768], P('chan', 'space'), may hold values from -0.1875 to 0.1875
- mix_out_bias: float32 [32768], P('space'), may hold values from -3 to 3
Outputs:
- mixed: bfloat16 [1, 1024, 32768], P(None, 'chan', 'space')
All inputs are finite; a program needn't handle non-finite values.
Results may differ from a plain program's by a relative error of at most 0.013.
Values may be sent and summed in bfloat16 or wider, within the bound.
A program may use at most 64 MiB of HBM per device.

v0:
```python
import jax
import jax.numpy as jnp
from jax import lax
from jax.sharding import PartitionSpec as P


def extended_2(shard, sides, width):
    for axis, dim in sides:
        count, length = (lax.axis_size(axis), shard.shape[dim])
        up = [(i, (i + 1) % count) for i in range(count - 1)]
        down = [(j, i) for i, j in up]
        last = lax.slice_in_dim(shard, length - width, length, axis=dim)
        first = lax.slice_in_dim(shard, 0, width, axis=dim)
        before = lax.ppermute(last, axis, up)
        after = lax.ppermute(first, axis, down)
        shard = jnp.concatenate([before, shard, after], axis=dim)
    return shard


def from_behind(value, axis, steps):
    count = lax.axis_size(axis)
    first, last = (max(0, -steps), min(count, count - steps))
    return lax.ppermute(value, axis, [(source, source + steps) for source in range(first, last)])


def convolve(inputs, filters, stride, padding):
    return lax.conv_general_dilated(
        inputs,
        filters,
        (stride, stride),
        padding,
        dimension_numbers=("NCHW", "HWIO", "NCHW"),
        preferred_element_type=jnp.float32,
    )


def shards(
    fields,
    stem_weight,
    stem_bias,
    embed_weight,
    embed_bias,
    norm_gain,
    norm_bias,
    mix_in,
    mix_in_bias,
    mix_out,
    mix_out_bias,
):
    height = fields.shape[2]
    breadth = fields.shape[3]
    padded = extended_2(fields, (("chan", 2), ("space", 3)), 1)
    stem_out = convolve(padded, stem_weight, 1, "VALID") + stem_bias[None, :, None, None]
    stem_out = jax.nn.gelu(stem_out, approximate=False).astype(jnp.bfloat16)
    upper = from_behind(stem_out[:, :, height - 3 :, :], "chan", 1)
    taller = jnp.concatenate([upper, stem_out], axis=2)
    leftward = from_behind(taller[:, :, :, breadth - 3 :], "space", 1)
    extended = jnp.concatenate([leftward, taller], axis=3)
    embedded = convolve(
        extended, lax.all_gather(embed_weight, "chan", axis=3, tiled=True), 4, "VALID"
    )
    embedded = (embedded + embed_bias[None, :, None, None]).astype(jnp.bfloat16)
    samples = embedded.shape[0]
    width = embedded.shape[1]
    local = width // lax.axis_size("chan")
    values = embedded.astype(jnp.float32)
    average = jnp.mean(values, axis=1, keepdims=True)
    variance = jnp.mean(values * values, axis=1, keepdims=True) - average * average
    normed_all = (values - average) * lax.rsqrt(variance + 1e-05) * norm_gain[
        None, :, None, None
    ] + norm_bias[None, :, None, None]
    normed_all = normed_all.astype(jnp.bfloat16)
    moved, normed = (
        lax.all_to_all(embedded, "chan", split_axis=1, concat_axis=2, tiled=True),
        lax.all_to_all(normed_all, "chan", split_axis=1, concat_axis=2, tiled=True),
    )
    token_rows = jnp.transpose(normed, (0, 1, 3, 2)).reshape(samples * local, -1)
    residual = jnp.transpose(moved, (0, 1, 3, 2)).reshape(samples * local, -1)
    partial_hidden = jnp.dot(
        token_rows,
        lax.all_gather(mix_in, "chan", axis=1, tiled=True),
        preferred_element_type=jnp.float32,
    )
    summed = lax.psum(partial_hidden.astype(jnp.bfloat16), "space").astype(jnp.float32)
    activated = jax.nn.gelu(summed + mix_in_bias[None, :], approximate=False).astype(jnp.bfloat16)
    initial = jnp.zeros((samples * local, mix_out.shape[1]), jnp.float32)
    output = initial + jnp.dot(
        activated,
        lax.all_gather(mix_out, "chan", axis=0, tiled=True),
        preferred_element_type=jnp.float32,
    )
    output = output + mix_out_bias[None, :]
    output = output + residual.astype(jnp.float32)
    return output.astype(jnp.bfloat16).reshape(samples, local, -1)


def solution(mesh):
    placed = (
        P(None, None, "chan", "space"),
        P(),
        P(),
        P(None, None, None, "chan"),
        P(),
        P(),
        P(),
        P("space", "chan"),
        P(),
        P("chan", "space"),
        P("space"),
    )
    return jax.shard_map(
        shards, mesh=mesh, in_specs=placed, out_specs=P(None, "chan", "space"), check_vma=False
    )
```

profile of v0, /device:TPU:4, one launch (start us, length us, event | category | flops | bytes accessed | tf_op | source)
XLA Modules:
  0.0 506.3 jit_solution(13815627416693066227)
XLA Ops:
  6.5 2.4 copy.106
  9.0 0.7 all-gather.6.cloned.1.call-update
  9.8 1.9 collective-permute-start
  11.7 3.6 collective-permute-start.1
  15.4 1.4 collective-permute-done.1
  16.8 0.1 pad_maximum_fusion
  16.9 0.1 fusion.118
  17.0 4.5 collective-permute-start.2
  21.5 1.3 collective-permute-start.3
  22.8 4.7 collective-permute-done.2
  27.5 9.8 %collective-permute-done.3 = bf16[1,20,34,1]{3,2,1,0:T(8,128)(2,1)S(1)} collective-permute-done((bf16[1,20,34,1]{3,2,1,0:T(8,128)(2,1)S(1)}, bf16[1,20,34,1]{3,2,1,0:T(8,128)(2,1)S(1)}, u32[]{:S(2)}, u32[]{:S(2)}) %collective-permute-start.3) | collective-permute-done | bytes 1392 | tf_op jit(solution)/shard_map/ppermute | solution.py:15
  37.3 0.3 maximum_bitcast_fusion
  37.5 0.3 copy.119
  37.8 0.1 pad.clone
  37.9 0.4 copy.101
  38.4 2.1 fusion.9
  40.5 0.1 slice_bitcast_fusion
  40.6 2.0 collective-permute-start.4
  42.7 0.5 copy.134
  43.3 3.9 collective-permute-done.4
  47.2 0.1 pad_maximum_fusion.1
  47.3 5.5 %collective-permute-start.5 = (bf16[1,32,35,3]{1,0,3,2:T(2,128)(2,1)S(1)}, bf16[1,32,35,3]{1,0,3,2:T(2,128)(2,1)S(1)}, u32[]{:S(2)}, u32[]{:S(2)}) collective-permute-start(bf16[1,32,35,3]{1,0,3,2:T(2,128)(2,1)S(1)} %pad_maximum_fusion.1), channel_id=1, source_target_pairs={{0,1},{1,2},{2,3},{3,4},{4,5},{5,6},{6,7},{7,8},{8,9},{9,10},{10,1... | collective-permute-start | bytes 20168 | tf_op jit(solution)/shard_map/ppermute | solution.py:23
  52.8 1.8 collective-permute-done.5
  54.6 46.1 %all-gather.4.cloned.1.call-done = bf16[7,7,32,1024]{2,1,0,3:T(8,128)(2,1)} async-done(((bf16[7,7,32,64]{2,1,0,3:T(8,128)(2,1)}), bf16[7,7,32,1024]{2,1,0,3:T(8,128)(2,1)}) %all-gather.4.cloned.1.call-update) | async-done | bytes 3211280 | tf_op jit(solution)/shard_map/all_gather | solution.py:60
  100.7 10.7 %fusion = f32[1,1024,8,8]{1,0,3,2:T(1,128)S(1)} fusion(bf16[7,7,32,1024]{2,1,0,3:T(8,128)(2,1)} %all-gather.4.cloned.1.call-done, bf16[1,32,32,32]{1,0,3,2:T(2,128)(2,1)S(1)} %bitcast.49, bf16[1,32,3,32]{1,0,3,2:T(2,128)(2,1)S(1)} %collective-permute-done.4, bf16[1,32,35,3]{1,0,3,2:T(2,128)(2,1)S(1)} %collective-permute-done.5), kind=kOutput, calls=%fused_computation | convolution fusion | flops 205756096 | bytes 3551808 | tf_op jit(solution)/shard_map/conv_general_dilated | solution.py:27
  111.4 0.1 convert_reduce_fusion
  111.6 0.1 fusion.32
  111.7 1.5 copy.109
  113.2 2.9 reshape.76
  116.1 10.7 %all-to-all-start = ((bf16[16,2,2048]{2,1,0:T(2,128)(2,1)}), bf16[16,2,2048]{2,1,0:T(2,128)(2,1)S(1)}, u32[]{:S(2)}, u32[]{:S(2)}) async-start(bf16[16,2,2048]{2,1,0:T(2,128)(2,1)} %reshape.76), calls=%async_computation | async-start | bytes 262144 | tf_op jit(solution)/shard_map/all_to_all | solution.py:75
  126.8 1.5 copy.113
  128.3 2.9 reshape.74
  131.1 0.3 all-to-all-done
  131.5 6.5 %all-to-all-start.1 = ((bf16[16,2,2048]{2,1,0:T(2,128)(2,1)}), bf16[16,2,2048]{2,1,0:T(2,128)(2,1)S(1)}, u32[]{:S(2)}, u32[]{:S(2)}) async-start(bf16[16,2,2048]{2,1,0:T(2,128)(2,1)} %reshape.74), calls=%async_computation.1 | async-start | bytes 262144 | tf_op jit(solution)/shard_map/all_to_all | solution.py:74
  138.1 2.5 reshape.77
  140.5 1.5 copy.117
  142.0 0.1 copy.111
  142.1 0.2 copy.112
  142.3 8.0 %all-gather.6.cloned.1.call-done = bf16[1024,1024]{0,1:T(8,128)(2,1)} async-done(((bf16[1024,64]{0,1:T(8,128)(2,1)}), bf16[1024,1024]{0,1:T(8,128)(2,1)}) %all-gather.6.cloned.1.call-update) | async-done | bytes 2097168 | tf_op jit(solution)/shard_map/all_gather | solution.py:81
  150.4 3.0 convolution_convert_fusion
  153.4 2.5 reshape.75
  155.9 1.4 copy.114
  157.3 0.1 reshape.72
  157.4 0.2 copy.115
  157.6 0.2 copy.116
  157.9 33.1 %all-gather.8.cloned.1.call-done = bf16[1024,1024]{1,0:T(8,128)(2,1)} async-done(((bf16[64,1024]{1,0:T(8,128)(2,1)}), bf16[1024,1024]{1,0:T(8,128)(2,1)}) %all-gather.8.cloned.1.call-update) | async-done | bytes 2097168 | tf_op jit(solution)/shard_map/all_gather | solution.py:89
  191.0 305.5 %all-reduce.2.cloned.1.call-done = bf16[64,1024]{1,0:T(8,128)(2,1)} async-done(((bf16[64,1024]{1,0:T(8,128)(2,1)}), bf16[64,1024]{1,0:T(8,128)(2,1)}) %all-reduce.2.cloned.1.call-update) | async-done | bytes 131088 | tf_op jit(solution)/shard_map/psum | solution.py:84
  496.5 3.3 fusion.5
  (35 shorter events, 0.4 us)
Async XLA Ops:
  6.5 31.8 %copy-start = (bf16[3,3,20,32]{3,2,1,0:T(8,128)(2,1)S(1)}, bf16[3,3,20,32]{3,2,1,0:T(8,128)(2,1)}, u32[]{:S(2)}) copy-start(bf16[3,3,20,32]{3,2,1,0:T(8,128)(2,1)} %param.12) | copy-start | bytes 34564
  6.5 3.2 copy-start.1
  6.5 94.2 %all-gather.4.cloned.1.call-start = ((), (), s32[]{:S(2)}) async-start(), calls=%async_computation.2 | async-start | bytes 15597568 | tf_op jit(solution)/shard_map/all_gather | solution.py:60
  9.0 29.4 %copy-start.7 = (f32[32]{0:T(128)S(1)}, f32[32]{0:T(128)}, u32[]{:S(2)}) copy-start(f32[32]{0:T(128)} %param.13) | copy-start | bytes 388
  9.0 29.4 %copy-start.8 = (pred[8,5]{0,1:T(8,128)(4,1)S(1)}, pred[8,5]{0,1:T(8,128)(4,1)}, u32[]{:S(2)}) copy-start(pred[8,5]{0,1:T(8,128)(4,1)} %constant.7) | copy-start | bytes 124
  9.0 141.4 %all-gather.6.cloned.1.call-start = ((), (), s32[]{:S(2)}) async-start(), calls=%async_computation.3 | async-start | bytes 2228224 | tf_op jit(solution)/shard_map/all_gather | solution.py:81
  9.7 181.2 %all-gather.8.cloned.1.call-start = ((), (), s32[]{:S(2)}) async-start(), calls=%async_computation.5 | async-start | bytes 2228224 | tf_op jit(solution)/shard_map/all_gather | solution.py:89
  9.8 5.6 %collective-permute-start = (bf16[1,20,1,32]{3,2,1,0:T(2,128)(2,1)S(1)}, bf16[1,20,1,32]{3,2,1,0:T(2,128)(2,1)S(1)}, u32[]{:S(2)}, u32[]{:S(2)}) collective-permute-start(bf16[1,20,1,32]{3,2,1,0:T(2,128)(2,1)S(1)} %get-tuple-element.10), channel_id=1, source_target_pairs={{0,32},{32,64},{64,96},{96,128},{128,160},{160,192},{192,224},{224... | collective-permute-start | bytes 3848 | tf_op jit(solution)/shard_map/ppermute | solution.py:14
  11.7 5.0 collective-permute-start.1
  17.0 10.5 %collective-permute-start.2 = (bf16[1,20,34,1]{3,2,1,0:T(8,128)(2,1)S(1)}, bf16[1,20,34,1]{3,2,1,0:T(8,128)(2,1)S(1)}, u32[]{:S(2)}, u32[]{:S(2)}) collective-permute-start(bf16[1,20,34,1]{3,2,1,0:T(8,128)(2,1)S(1)} %get-tuple-element.8), channel_id=1, source_target_pairs={{0,1},{1,2},{2,3},{3,4},{4,5},{5,6},{6,7},{7,8},{8,9},{9,10},{10,1... | collective-permute-start | bytes 4088 | tf_op jit(solution)/shard_map/ppermute | solution.py:14
  21.5 15.8 %collective-permute-start.3 = (bf16[1,20,34,1]{3,2,1,0:T(8,128)(2,1)S(1)}, bf16[1,20,34,1]{3,2,1,0:T(8,128)(2,1)S(1)}, u32[]{:S(2)}, u32[]{:S(2)}) collective-permute-start(bf16[1,20,34,1]{3,2,1,0:T(8,128)(2,1)S(1)} %get-tuple-element.9), channel_id=1, source_target_pairs={{1,0},{2,1},{3,2},{4,3},{5,4},{6,5},{7,6},{8,7},{9,8},{10,9},{11,1... | collective-permute-start | bytes 4088 | tf_op jit(solution)/shard_map/ppermute | solution.py:15
  40.6 6.6 %collective-permute-start.4 = (bf16[1,32,3,32]{1,0,3,2:T(2,128)(2,1)S(1)}, bf16[1,32,3,32]{1,0,3,2:T(2,128)(2,1)S(1)}, u32[]{:S(2)}, u32[]{:S(2)}) collective-permute-start(bf16[1,32,3,32]{1,0,3,2:T(2,128)(2,1)S(1)} %slice_bitcast_fusion), channel_id=1, source_target_pairs={{0,32},{32,64},{64,96},{96,128},{128,160},{160,192},{192,224},{224... | collective-permute-start | bytes 18440 | tf_op jit(solution)/shard_map/ppermute | solution.py:23
  47.2 64.1 %copy-start.2 = (f32[1024]{0:T(1024)S(1)}, f32[1024]{0:T(1024)}, u32[]{:S(2)}) copy-start(f32[1024]{0:T(1024)} %param.15) | copy-start | bytes 12292
  47.3 64.3 %copy-start.3 = (f32[1024]{0:T(1024)S(1)}, f32[1024]{0:T(1024)}, u32[]{:S(2)}) copy-start(f32[1024]{0:T(1024)} %param.17) | copy-start | bytes 12292
  47.3 64.3 %copy-start.4 = (f32[1024]{0:T(1024)S(1)}, f32[1024]{0:T(1024)}, u32[]{:S(2)}) copy-start(f32[1024]{0:T(1024)} %param.16) | copy-start | bytes 12292
  47.3 7.3 %collective-permute-start.5 = (bf16[1,32,35,3]{1,0,3,2:T(2,128)(2,1)S(1)}, bf16[1,32,35,3]{1,0,3,2:T(2,128)(2,1)S(1)}, u32[]{:S(2)}, u32[]{:S(2)}) collective-permute-start(bf16[1,32,35,3]{1,0,3,2:T(2,128)(2,1)S(1)} %pad_maximum_fusion.1), channel_id=1, source_target_pairs={{0,1},{1,2},{2,3},{3,4},{4,5},{5,6},{6,7},{7,8},{8,9},{9,10},{10,1... | collective-permute-start | bytes 20168 | tf_op jit(solution)/shard_map/ppermute | solution.py:23
  116.1 15.4 %all-to-all-start = ((bf16[16,2,2048]{2,1,0:T(2,128)(2,1)}), bf16[16,2,2048]{2,1,0:T(2,128)(2,1)S(1)}, u32[]{:S(2)}, u32[]{:S(2)}) async-start(bf16[16,2,2048]{2,1,0:T(2,128)(2,1)} %reshape.76), calls=%async_computation | async-start | bytes 262144 | tf_op jit(solution)/shard_map/all_to_all | solution.py:75
  131.5 21.9 %all-to-all-start.1 = ((bf16[16,2,2048]{2,1,0:T(2,128)(2,1)}), bf16[16,2,2048]{2,1,0:T(2,128)(2,1)S(1)}, u32[]{:S(2)}, u32[]{:S(2)}) async-start(bf16[16,2,2048]{2,1,0:T(2,128)(2,1)} %reshape.74), calls=%async_computation.1 | async-start | bytes 262144 | tf_op jit(solution)/shard_map/all_to_all | solution.py:74
  138.0 358.5 %all-reduce.2.cloned.1.call-start = ((), (), s32[]{:S(2)}) async-start(), calls=%async_computation.4 | async-start | bytes 262144 | tf_op jit(solution)/shard_map/psum | solution.py:84
  155.9 340.6 %copy-start.5 = (f32[1024]{0:T(1024)S(1)}, f32[1024]{0:T(1024)}, u32[]{:S(2)}) copy-start(f32[1024]{0:T(1024)} %param.21) | copy-start | bytes 12292
  155.9 340.6 %copy-start.6 = (f32[1024]{0:T(1024)S(1)}, f32[1024]{0:T(1024)}, u32[]{:S(2)}) copy-start(f32[1024]{0:T(1024)} %param.19) | copy-start | bytes 12292
Sparse Core Ops, SparseCore 0:
  9.5 91.2 all-gather.3
  102.9 47.4 all-gather.5
  152.5 38.4 all-gather.7
  193.7 302.7 all-reduce.1
where the time goes:
time: 507 us; the launch traced here: 506 us
  waiting for transfers between devices  415 us (82%)
  starting transfers between devices  36.3 us (7%)
  local copies, waits for them, and re-layouts  21.5 us (4%)
  matrix products  19 us (4%)
  between operations  13.5 us (3%)
    psum x1, waiting for transfers between devices, shards(): lax.psum(partial_hidden.astype(jnp.bfloat16), 'space').astype(jnp.float32)  306 us
    all_gather x1, waiting for transfers between devices, shards(): lax.all_gather(embed_weight, 'chan', axis=3, tiled=True)  46.1 us
    all_gather x1, waiting for transfers between devices, shards(): lax.all_gather(mix_out, 'chan', axis=0, tiled=True)  33.1 us
    unnamed x25, local copies, waits for them, and re-layouts  13.9 us
    conv_general_dilated x2, matrix products, convolve(): lax.conv_general_dilated(inputs, filters, (stride, stride), padding, dime...  12.7 us
    ppermute x2, waiting for transfers between devices, extended_2(): after = lax.ppermute(first, axis, down)  11.1 us
    all_to_all x1, starting transfers between devices, shards(): lax.all_to_all(normed_all, 'chan', split_axis=1, concat_axis=2, tiled=True)  10.7 us
  transfers between devices with their start and end apart: 12, of which 10 were waited for; matrix products, arithmetic and copies ran while one was open for 7% of the time, Pallas kernels for 0%

commit v1 on v0

v1 whole, which is shorter than its diff:
```python
import functools

import jax
import jax.numpy as jnp
from jax import lax
from jax.experimental import pallas as pl
from jax.experimental.pallas import tpu as pltpu
from jax.sharding import PartitionSpec as P

MESH = pl.DeviceIdType.MESH
CHIPS = 8
SPACE = 32
F32 = jnp.float32
BF16 = jnp.bfloat16


def gelu(x):
    return 0.5 * x * (1.0 + lax.erf(x * 0.7071067811865476))


def kernel(
    t1_ref,
    tw_ref,
    sb_ref,
    w_ref,
    eb_ref,
    gn_ref,
    nb_ref,
    mi_ref,
    mb_ref,
    mo_ref,
    ob_ref,
    out_ref,
    aext,
    gc,
    rv,
    rh,
    rd,
    xall,
    wall,
    eh,
    st,
    mi_all,
    mo_all,
    hs,
    rs,
    act,
    po,
    pr,
    halo_send,
    halo_recv,
    send,
    recv,
    local,
):
    c, s = lax.axis_index("chan"), lax.axis_index("space")
    k, core = c // 2, c % 2
    other = 1 - core
    partner = (2 * k + other, s)
    right, left = (s + 1) % SPACE, (s + SPACE - 1) % SPACE
    side = jnp.where(core == 0, left, right)

    def remote(src, dst, ssem, rsem, to):
        copy = pltpu.make_async_remote_copy(
            src_ref=src, dst_ref=dst, send_sem=ssem, recv_sem=rsem, device_id=to, device_id_type=MESH
        )
        copy.start()

    def wait(ref, sem):
        pltpu.make_async_copy(ref, ref, sem).wait()

    def peer(d):
        return (2 * ((k + d) % CHIPS) + core, s)

    barrier = pltpu.get_barrier_semaphore()

    def greet(to):
        pl.semaphore_signal(barrier, inc=1, device_id=to, device_id_type=MESH)

    @pl.loop(1, 16)
    def _(d):
        greet(((c + d) % 16, s))

    @pl.loop(1, SPACE)
    def _(d):
        greet((c, (s + d) % SPACE))

    greet((2 * k + other, side))
    greet(((2 * k + 15) % 16, side))
    greet(((2 * k + 2) % 16, side))

    for slot in range(10):
        base = slot * 80 // 128 * 128
        window = t1_ref[:, base : base + 256]
        shift = slot * 80 - base
        if shift:
            window = pltpu.roll(window, 256 - shift, axis=1)
        window = window[:, :128]
        for row in range(4):
            aext[row, slot] = window[8 * row : 8 * row + 8]

    pl.semaphore_wait(barrier, 49)

    own_rows = pl.ds(pl.multiple_of(8 * core, 8), 8)
    edge = 3 * core
    below = (k + 2 * core + CHIPS - 1) % CHIPS
    remote(
        aext.at[:, pl.ds(4 * other, 5)], gc.at[:, :, own_rows], halo_send.at[0], halo_recv.at[0], partner
    )
    for to in range(2):
        remote(
            aext.at[edge, pl.ds(4 * to, 5)],
            rv.at[other],
            halo_send.at[1 + to],
            halo_recv.at[1 + other],
            (2 * below + to, s),
        )
        away = right if to == 0 else left
        start = 8 - 8 * to
        remote(
            aext.at[:, start : start + 2],
            rh.at[core],
            halo_send.at[3 + to],
            halo_recv.at[3 + core],
            (2 * k + to, away),
        )
        remote(
            aext.at[edge, start : start + 2],
            rd.at[other],
            halo_send.at[5 + to],
            halo_recv.at[5 + other],
            (2 * below + to, away),
        )
    remote(w_ref, wall.at[core], send.at[0], recv.at[0], partner)
    own_w = pltpu.make_async_copy(w_ref, wall.at[core], local.at[0])
    own_w.start()
    lanes_k = pl.ds(pl.multiple_of(128 * k, 128), 128)
    own_mi = pltpu.make_async_copy(mi_ref, mi_all.at[:, lanes_k], local.at[1])
    own_mi.start()
    rows_k = pl.ds(pl.multiple_of(64 * k, 64), 64)
    own_mo = pltpu.make_async_copy(mo_ref, mo_all.at[rows_k], local.at[2])
    own_mo.start()

    @pl.loop(1, CHIPS)
    def _(d):
        remote(mi_ref, mi_all.at[:, lanes_k], send.at[1], recv.at[1], peer(d))

    gc[:, :, own_rows] = aext[:, pl.ds(4 * core, 5)]
    wait(gc.at[:, :, own_rows], halo_recv.at[0])
    for i in range(2):
        wait(rv.at[i], halo_recv.at[1 + i])
        wait(rh.at[i], halo_recv.at[3 + i])
        wait(rd.at[i], halo_recv.at[5 + i])
    at_left = jnp.logical_and(core == 0, s > 0)
    at_right = jnp.logical_and(core == 1, s < SPACE - 1)
    for half in range(2):
        rows = slice(8 * half, 8 * half + 8)
        for row in range(4):
            for slot, use, column in ((0, at_left, 0), (1, at_left, 1), (4, at_right, 0)):
                gc[row, slot, rows] += jnp.where(use, rh[half, row, column], 0.0)
    beyond = []
    for half, inside in ((0, k > 0), (1, k < CHIPS - 1)):
        slabs = []
        for slot in range(5):
            value = rv[half, slot]
            if slot in (0, 1):
                value = value + jnp.where(at_left, rd[half, slot], 0.0)
            if slot == 4:
                value = value + jnp.where(at_right, rd[half, 0], 0.0)
            value = jnp.where(inside, value, 0.0)
            value = value[7:8] if half == 0 else value[0:1]
            slabs.append(jnp.broadcast_to(value, (16, 128)))
        beyond.append(jnp.concatenate(slabs, axis=0))
    grid = [gc[row].reshape(80, 128) for row in range(4)]
    place = lax.broadcasted_iota(jnp.int32, (80, 128), 0) % 16
    before = jnp.where(place == 0, beyond[0], pltpu.roll(grid[3], 1, axis=0))
    after = jnp.where(place == 15, beyond[1], pltpu.roll(grid[0], 79, axis=0))
    lines = [line.astype(BF16) for line in (before, *grid, after)]
    outside = jnp.logical_and(core == 0, s == 0)
    keep = jnp.logical_or(lax.broadcasted_iota(jnp.int32, (80, 128), 0) >= 16, jnp.logical_not(outside))
    rows16 = pl.ds(pl.multiple_of(16 * k, 16), 16)
    for row in range(4):
        patches = jnp.concatenate(lines[row : row + 3], axis=1)
        stem = jnp.dot(patches, tw_ref[...], preferred_element_type=F32) + sb_ref[...]
        stem = jnp.where(keep, gelu(stem), 0.0)
        xall[:, rows16, 128 * row : 128 * row + 128] = stem.reshape(5, 16, 128).astype(BF16)

    @pl.loop(1, CHIPS)
    def _(d):
        remote(xall.at[:, rows16], xall.at[:, rows16], send.at[2], recv.at[2], peer(d))

    @pl.loop(1, CHIPS)
    def _(d):
        remote(mo_ref, mo_all.at[rows_k], send.at[3], recv.at[3], peer(d))

    own_w.wait()
    wait(w_ref, recv.at[0])
    wait(xall.at[:, :112], recv.at[2])
    tokens = xall[...].reshape(640, 512)
    lane = lax.broadcasted_iota(jnp.int32, (64, 128), 1)
    sums = [[0.0, 0.0] for _ in range(4)]
    for half in range(2):
        terms = jnp.dot(tokens, wall[half], preferred_element_type=F32)
        both = terms[128:640, 128:256] + terms[0:512, 0:128] + eb_ref[pl.ds(2 * k + half, 1), :]
        for column in range(4):
            turned = both[128 * column : 128 * column + 128].T
            shifted = pltpu.roll(turned[0:64], 1, axis=1)
            value = (turned[64:128] + jnp.where(lane > 0, shifted, 0.0)).astype(BF16)
            eh[core, 64 * half : 64 * half + 64, 128 * column : 128 * column + 128] = value
            wide = value.astype(F32)
            sums[column][0] += jnp.sum(wide, axis=0, keepdims=True)
            sums[column][1] += jnp.sum(wide * wide, axis=0, keepdims=True)
    for column in range(4):
        for kind in range(2):
            st[c, kind : kind + 1, 128 * column : 128 * column + 128] = sums[column][kind]

    @pl.loop(1, 16)
    def _(d):
        remote(st.at[c], st.at[c], send.at[4], recv.at[4], ((c + d) % 16, s))

    remote(eh.at[core], eh.at[core], send.at[5], recv.at[5], partner)

    gain = jnp.broadcast_to(gn_ref[pl.ds(k, 1), :], (128, 128)).T
    offset = jnp.broadcast_to(nb_ref[pl.ds(k, 1), :], (128, 128)).T
    gain = jnp.concatenate([gain] * 4, axis=1)
    offset = jnp.concatenate([offset] * 4, axis=1)
    wait(st.at[:15], recv.at[4])
    wait(eh.at[0], recv.at[5])
    normed = []
    for half in range(2):
        total = st[half]
        for chip in range(1, CHIPS):
            total = total + st[2 * chip + half]
        average = total[0:1] * (1.0 / 1024)
        variance = total[1:2] * (1.0 / 1024) - average * average
        scale = lax.rsqrt(variance + 1e-05)
        value = (eh[half].astype(F32) - average) * scale * gain + offset
        normed.append(value.astype(BF16))
    normed = jnp.concatenate(normed, axis=0)

    own_mi.wait()
    wait(mi_all.at[:, :896], recv.at[1])
    low = lax.broadcasted_iota(jnp.int32, (128, 128), 1) < 64
    for block in range(4):
        part = jnp.dot(normed, mi_all[:, 256 * block : 256 * block + 256], preferred_element_type=F32)
        first = part[0:128, 0:128] + pltpu.roll(part[128:256, 0:128], 64, axis=1)
        second = pltpu.roll(part[0:128, 128:256], 64, axis=1) + part[128:256, 128:256]
        summed = jnp.where(low, first, second).astype(BF16)
        for band in range(8):
            hs[4 * band + block] = summed[16 * band : 16 * band + 16]

    @pl.loop(1, SPACE)
    def _(d):
        to = (s + d) % SPACE
        remote(hs.at[to], rs.at[s], send.at[6], recv.at[6], (c, to))

    rs[s] = hs[s]
    wait(rs.at[: SPACE - 1], recv.at[6])
    total = rs[0].astype(F32)
    for source in range(1, SPACE):
        total = total + rs[source].astype(F32)
    total = total + mb_ref[core, pl.ds(s % 4, 1), :]
    act[s] = gelu(total).astype(BF16)

    @pl.loop(1, SPACE)
    def _(d):
        remote(act.at[s], act.at[s], send.at[7], recv.at[7], (c, (s + d) % SPACE))

    own_mo.wait()
    wait(mo_all.at[:448], recv.at[3])
    wait(act.at[: SPACE - 1], recv.at[7])

    def rows_of(which):
        blocks = act[pl.ds(16 * which, 16)]
        lines = [jnp.concatenate([blocks[4 * band + lb] for lb in range(4)], axis=1) for band in range(4)]
        return jnp.concatenate(lines, axis=0)

    po[...] = jnp.dot(rows_of(other), mo_all[...], preferred_element_type=F32)
    remote(po, pr, send.at[8], recv.at[8], partner)
    mine = jnp.dot(rows_of(core), mo_all[...], preferred_element_type=F32) + ob_ref[...]
    residual = [eh[half, pl.ds(pl.multiple_of(64 * core, 64), 64), :].astype(F32) for half in range(2)]
    mine = mine + jnp.concatenate(residual, axis=1)
    wait(pr, recv.at[8])
    out_ref[...] = (mine + pr[...]).astype(BF16)

    wait(gc.at[:, :, own_rows], halo_send.at[0])
    for i in range(2):
        wait(rv.at[i], halo_send.at[1 + i])
        wait(rh.at[i], halo_send.at[3 + i])
        wait(rd.at[i], halo_send.at[5 + i])
    wait(w_ref, send.at[0])
    wait(mi_all.at[:, :896], send.at[1])
    wait(xall.at[:, :112], send.at[2])
    wait(mo_all.at[:448], send.at[3])
    wait(st.at[:15], send.at[4])
    wait(eh.at[0], send.at[5])
    wait(rs.at[: SPACE - 1], send.at[6])
    wait(act.at[: SPACE - 1], send.at[7])
    wait(po, send.at[8])


def shards(
    fields,
    stem_weight,
    stem_bias,
    embed_weight,
    embed_bias,
    norm_gain,
    norm_bias,
    mix_in,
    mix_in_bias,
    mix_out,
    mix_out_bias,
):
    t1 = fields[0].astype(F32).reshape(20, 8, 4, 32).transpose(2, 1, 3, 0).reshape(32, 640)
    t1 = jnp.pad(t1, ((0, 0), (100, 156)))
    tw = jnp.stack([jnp.pad(stem_weight, ((0, 0), (i, 3 - i), (0, 0), (0, 0))) for i in range(4)], axis=3)
    tw = jnp.pad(tw.reshape(3, 120, 128), ((0, 0), (0, 8), (0, 0))).reshape(384, 128)
    sb = jnp.tile(stem_bias, 4)[None]
    w = jnp.pad(embed_weight, ((1, 0), (1, 0), (0, 0), (0, 0))).reshape(2, 4, 2, 4, 32, 64)
    w = w.transpose(1, 3, 4, 2, 0, 5).reshape(512, 256)
    eb = jnp.pad(embed_bias.reshape(16, 64), ((0, 0), (64, 0)))
    mi = jnp.concatenate([mix_in[:512], mix_in[512:]], axis=1)
    mb = mix_in_bias.reshape(8, 2, 64).transpose(1, 0, 2).reshape(2, 4, 128)
    out = pl.pallas_call(
        kernel,
        out_shape=jax.ShapeDtypeStruct((64, 1024), BF16),
        in_specs=[pl.BlockSpec(memory_space=pltpu.VMEM)] * 11,
        out_specs=pl.BlockSpec(memory_space=pltpu.VMEM),
        scratch_shapes=[
            pltpu.VMEM((4, 10, 8, 128), F32),
            pltpu.VMEM((4, 5, 16, 128), F32),
            pltpu.VMEM((2, 5, 8, 128), F32),
            pltpu.VMEM((2, 4, 2, 8, 128), F32),
            pltpu.VMEM((2, 2, 8, 128), F32),
            pltpu.VMEM((5, 128, 512), BF16),
            pltpu.VMEM((2, 512, 256), BF16),
            pltpu.VMEM((2, 128, 512), BF16),
            pltpu.VMEM((16, 2, 512), F32),
            pltpu.VMEM((512, 1024), BF16),
            pltpu.VMEM((512, 1024), BF16),
            pltpu.VMEM((SPACE, 16, 128), BF16),
            pltpu.VMEM((SPACE, 16, 128), BF16),
            pltpu.VMEM((SPACE, 16, 128), BF16),
            pltpu.VMEM((64, 1024), F32),
            pltpu.VMEM((64, 1024), F32),
            pltpu.SemaphoreType.DMA((7,)),
            pltpu.SemaphoreType.DMA((7,)),
            pltpu.SemaphoreType.DMA((9,)),
            pltpu.SemaphoreType.DMA((9,)),
            pltpu.SemaphoreType.DMA((3,)),
        ],
        compiler_params=pltpu.CompilerParams(collective_id=0, has_side_effects=True),
    )(
        t1,
        tw,
        sb,
        w,
        eb,
        norm_gain.reshape(8, 128),
        norm_bias.reshape(8, 128),
        mi,
        mb,
        mix_out,
        mix_out_bias[None],
    )
    return out[None]


def solution(mesh):
    placed = (
        P(None, None, "chan", "space"),
        P(),
        P(),
        P(None, None, None, "chan"),
        P(),
        P(),
        P(),
        P("space", "chan"),
        P(),
        P("chan", "space"),
        P("space"),
    )
    return jax.shard_map(
        shards, mesh=mesh, in_specs=placed, out_specs=P(None, "chan", "space"), check_vma=False
    )
```

time: 507 us -> 86.4 us (0.17)
  the two profiles are of different devices: /device:TPU:4 before, /device:TPU:1 now
where the time goes in v1:
time: 86.4 us; the launch traced here: 86.1 us
  Pallas kernels  75.4 us (87%)
  local copies, waits for them, and re-layouts  8.95 us (10%)
  other arithmetic  1.64 us (2%)
    pallas_call x1, Pallas kernels, shards(): pl.pallas_call(kernel, out_shape=jax.ShapeDtypeStruct((64, 1024), BF16),...  75.4 us
    unnamed x15, local copies, waits for them, and re-layouts  2.57 us

profile of v1, /device:TPU:1, one launch (start us, length us, event | category | flops | bytes accessed | tf_op | source)
XLA Modules:
  0.0 86.1 jit_solution(11614761137350614413)
XLA Ops:
  0.0 1.2 %copy.16 = bf16[20,8,4,32]{0,3,1,2:T(8,128)(2,1)S(1)} copy(bf16[20,8,4,32]{3,2,1,0:T(4,128)(2,1)} %bitcast.27) | data formatting | bytes 81920 | tf_op jit(solution)/shard_map/convert_element_type | solution.py:315
  1.2 0.3 reshape.36
  1.6 0.0 copy-start.2
  1.6 0.7 pad_convert_fusion.t1_ref
  2.3 0.1 copy-done.2
  2.4 0.1 pad_bitcast_fusion.3
  2.5 0.1 pad_maximum_fusion
  2.6 0.1 copy.17
  2.8 0.0 copy-start
  2.8 0.2 reshape.37
  3.0 0.6 pad.40
  3.6 0.0 copy-start.5
  3.6 0.7 copy-done.5
  4.3 0.6 broadcast_in_dim_tile.3.sb_ref
  4.9 0.0 copy-done
  4.9 0.1 pad.41
  5.0 0.5 copy.25
  5.5 0.0 copy-start.3
  5.5 0.0 copy-start.1
  5.5 1.0 %reshape.40.w_ref = bf16[512,256]{1,0:T(8,128)(2,1)} reshape(bf16[4,4,32,2,2,64]{5,4,3,2,1,0:T(2,128)(2,1)S(1)} %bitcast.23) | data formatting | bytes 524288 | tf_op jit(solution)/shard_map/reshape | solution.py:321
  6.6 0.0 copy-done.3
  6.6 0.1 reshape.41
  6.7 0.7 pad.42.eb_ref
  7.3 0.0 copy-done.1
  7.3 0.1 copy.23
  7.5 0.1 copy.22
  7.6 0.0 copy-start.4
  7.6 0.8 pad_maximum_fusion.1.mi_ref
  8.4 0.0 copy-done.4
  8.4 0.1 reshape.44
  8.5 0.7 reshape.45.mb_ref
  9.1 75.4 %shard_map.109 = bf16[64,1024]{1,0:T(8,128)(2,1)} custom-call(f32[32,896]{1,0:T(8,128)} %pad_convert_fusion.t1_ref, bf16[384,128]{1,0:T(8,128)(2,1)} %bitcast.26, f32[1,128]{1,0:T(1,128)} %broadcast_in_dim_tile.3.sb_ref, bf16[512,256]{1,0:T(8,128)(2,1)} %reshape.40.w_ref, f32[16,128]{1,0:T(8,128)} %pad.42.eb_ref, f32[8,128]{1,0:T(8,128)} %bitcast.29, ...), custom_call_target="tpu_custom_call" | custom-call | tf_op jit(solution)/shard_map/pallas_call | solution.py:325
  84.6 1.6 %copy.27 = bf16[1,64,1024]{2,1,0:T(8,128)(2,1)} copy(bf16[1,64,1024]{2,1,0:T(8,128)(2,1)} %bitcast.25) | data formatting | bytes 262144
  (3 shorter events, 0.0 us)
Async XLA Ops:
  1.6 0.8 copy-start.2
  2.8 2.1 %copy-start = (bf16[7,7,32,64]{3,2,1,0:T(8,128)(2,1)S(1)}, bf16[7,7,32,64]{3,2,1,0:T(8,128)(2,1)}, u32[]{:S(2)}) copy-start(bf16[7,7,32,64]{3,2,1,0:T(8,128)(2,1)} %param.14) | copy-start | bytes 602116
  3.6 0.7 copy-start.5
  5.5 1.1 %copy-start.3 = (f32[1024]{0:T(1024)S(1)}, f32[1024]{0:T(1024)}, u32[]{:S(2)}) copy-start(f32[1024]{0:T(1024)} %param.15) | copy-start | bytes 12292
  5.5 1.8 %copy-start.1 = (bf16[1024,64]{0,1:T(8,128)(2,1)S(1)}, bf16[1024,64]{0,1:T(8,128)(2,1)}, u32[]{:S(2)}) copy-start(bf16[1024,64]{0,1:T(8,128)(2,1)} %param.18) | copy-start | bytes 393220
  7.6 0.8 copy-start.4

commit v2 on v1

--- a/solution.py
+++ b/solution.py
@@ -44,6 +44,7 @@
     mo_all,
     hs,
     rs,
+    quarter,
     act,
     po,
     pr,
@@ -57,6 +58,7 @@
     k, core = c // 2, c % 2
     other = 1 - core
     partner = (2 * k + other, s)
+    z, part = s // 4, s % 4
     right, left = (s + 1) % SPACE, (s + SPACE - 1) % SPACE
     side = jnp.where(core == 0, left, right)
 
@@ -69,8 +71,33 @@
     def wait(ref, sem):
         pltpu.make_async_copy(ref, ref, sem).wait()
 
-    def peer(d):
-        return (2 * ((k + d) % CHIPS) + core, s)
+    ring, x = k // 4, k % 4
+    ahead, behind = (x + 1) % 4, (x + 3) % 4
+
+    def chip(r, i):
+        return (2 * (4 * r + i) + core, s)
+
+    near = [chip(ring, ahead), chip(ring, behind), chip(1 - ring, x), chip(1 - ring, ahead), chip(1 - ring, behind)]
+
+    def spread(src, dst, ssem, rsem):
+        for to in near:
+            remote(src, dst, ssem, rsem, to)
+
+    def forward(half, ssem, rsem):
+        for r in range(2):
+            passed = half(4 * r + behind, 0)
+            remote(passed, passed, ssem, rsem, chip(ring, ahead))
+            passed = half(4 * r + ahead, 1)
+            remote(passed, passed, ssem, rsem, chip(ring, behind))
+
+    def mi_half(owner, which):
+        return mi_all.at[256 * which : 256 * which + 256, pl.ds(pl.multiple_of(128 * owner, 128), 128)]
+
+    def mo_half(owner, which):
+        return mo_all.at[pl.ds(pl.multiple_of(64 * owner + 32 * which, 32), 32)]
+
+    def x_half(owner, which):
+        return xall.at[:, pl.ds(pl.multiple_of(16 * owner, 16), 16), 256 * which : 256 * which + 256]
 
     barrier = pltpu.get_barrier_semaphore()
 
@@ -81,10 +108,13 @@
     def _(d):
         greet(((c + d) % 16, s))
 
-    @pl.loop(1, SPACE)
+    @pl.loop(1, 8)
     def _(d):
-        greet((c, (s + d) % SPACE))
-
+        greet((c, (s + 4 * d) % SPACE))
+
+    for d in range(1, 4):
+        greet((c, 4 * z + (part + d) % 4))
+    greet((c, side))
     greet((2 * k + other, side))
     greet(((2 * k + 15) % 16, side))
     greet(((2 * k + 2) % 16, side))
@@ -99,7 +129,7 @@
         for row in range(4):
             aext[row, slot] = window[8 * row : 8 * row + 8]
 
-    pl.semaphore_wait(barrier, 49)
+    pl.semaphore_wait(barrier, 29)
 
     own_rows = pl.ds(pl.multiple_of(8 * core, 8), 8)
     edge = 3 * core
@@ -141,9 +171,7 @@
     own_mo = pltpu.make_async_copy(mo_ref, mo_all.at[rows_k], local.at[2])
     own_mo.start()
 
-    @pl.loop(1, CHIPS)
-    def _(d):
-        remote(mi_ref, mi_all.at[:, lanes_k], send.at[1], recv.at[1], peer(d))
+    spread(mi_ref, mi_all.at[:, lanes_k], send.at[1], recv.at[1])
 
     gc[:, :, own_rows] = aext[:, pl.ds(4 * core, 5)]
     wait(gc.at[:, :, own_rows], halo_recv.at[0])
@@ -185,17 +213,16 @@
         stem = jnp.where(keep, gelu(stem), 0.0)
         xall[:, rows16, 128 * row : 128 * row + 128] = stem.reshape(5, 16, 128).astype(BF16)
 
-    @pl.loop(1, CHIPS)
-    def _(d):
-        remote(xall.at[:, rows16], xall.at[:, rows16], send.at[2], recv.at[2], peer(d))
-
-    @pl.loop(1, CHIPS)
-    def _(d):
-        remote(mo_ref, mo_all.at[rows_k], send.at[3], recv.at[3], peer(d))
+    spread(xall.at[:, rows16], xall.at[:, rows16], send.at[2], recv.at[2])
+
+    wait(xall.at[:, :80], recv.at[2])
+    forward(x_half, send.at[9], recv.at[9])
+    wait(mi_all.at[:, :640], recv.at[1])
+    forward(mi_half, send.at[10], recv.at[10])
 
     own_w.wait()
     wait(w_ref, recv.at[0])
-    wait(xall.at[:, :112], recv.at[2])
+    wait(xall.at[:, :32], recv.at[9])
     tokens = xall[...].reshape(640, 512)
     lane = lax.broadcasted_iota(jnp.int32, (64, 128), 1)
     sums = [[0.0, 0.0] for _ in range(4)]
@@ -226,11 +253,12 @@
     offset = jnp.concatenate([offset] * 4, axis=1)
     wait(st.at[:15], recv.at[4])
     wait(eh.at[0], recv.at[5])
+    spread(mo_ref, mo_all.at[rows_k], send.at[3], recv.at[3])
     normed = []
     for half in range(2):
         total = st[half]
-        for chip in range(1, CHIPS):
-            total = total + st[2 * chip + half]
+        for j in range(1, CHIPS):
+            total = total + st[2 * j + half]
         average = total[0:1] * (1.0 / 1024)
         variance = total[1:2] * (1.0 / 1024) - average * average
         scale = lax.rsqrt(variance + 1e-05)
@@ -239,41 +267,49 @@
     normed = jnp.concatenate(normed, axis=0)
 
     own_mi.wait()
-    wait(mi_all.at[:, :896], recv.at[1])
+    wait(mi_all.at[:, :256], recv.at[10])
     low = lax.broadcasted_iota(jnp.int32, (128, 128), 1) < 64
     for block in range(4):
-        part = jnp.dot(normed, mi_all[:, 256 * block : 256 * block + 256], preferred_element_type=F32)
-        first = part[0:128, 0:128] + pltpu.roll(part[128:256, 0:128], 64, axis=1)
-        second = pltpu.roll(part[0:128, 128:256], 64, axis=1) + part[128:256, 128:256]
+        prod = jnp.dot(normed, mi_all[:, 256 * block : 256 * block + 256], preferred_element_type=F32)
+        first = prod[0:128, 0:128] + pltpu.roll(prod[128:256, 0:128], 64, axis=1)
+        second = pltpu.roll(prod[0:128, 128:256], 64, axis=1) + prod[128:256, 128:256]
         summed = jnp.where(low, first, second).astype(BF16)
         for band in range(8):
-            hs[4 * band + block] = summed[16 * band : 16 * band + 16]
-
-    @pl.loop(1, SPACE)
+            hs[band, :, 128 * block : 128 * block + 128] = summed[16 * band : 16 * band + 16]
+
+    @pl.loop(1, 8)
     def _(d):
-        to = (s + d) % SPACE
-        remote(hs.at[to], rs.at[s], send.at[6], recv.at[6], (c, to))
-
-    rs[s] = hs[s]
-    wait(rs.at[: SPACE - 1], recv.at[6])
+        to = (z + d) % 8
+        remote(hs.at[to], rs.at[z], send.at[6], recv.at[6], (c, 4 * to + part))
+
+    rs[z] = hs[z]
+    wait(rs.at[:7], recv.at[6])
     total = rs[0].astype(F32)
-    for source in range(1, SPACE):
+    for source in range(1, 8):
         total = total + rs[source].astype(F32)
-    total = total + mb_ref[core, pl.ds(s % 4, 1), :]
-    act[s] = gelu(total).astype(BF16)
-
-    @pl.loop(1, SPACE)
+    quarter[part] = total.astype(BF16)
+    for d in range(1, 4):
+        to = 4 * z + (part + d) % 4
+        remote(quarter.at[part], quarter.at[part], send.at[7], recv.at[7], (c, to))
+    wait(mo_all.at[:320], recv.at[3])
+    forward(mo_half, send.at[11], recv.at[11])
+    wait(quarter.at[:3], recv.at[7])
+    total = quarter[0].astype(F32)
+    for source in range(1, 4):
+        total = total + quarter[source].astype(F32)
+    total = total + mb_ref[pl.ds(core, 1), :]
+    act[z] = gelu(total).astype(BF16)
+
+    @pl.loop(1, 8)
     def _(d):
-        remote(act.at[s], act.at[s], send.at[7], recv.at[7], (c, (s + d) % SPACE))
+        remote(act.at[z], act.at[z], send.at[12], recv.at[12], (c, (s + 4 * d) % SPACE))
 
     own_mo.wait()
-    wait(mo_all.at[:448], recv.at[3])
-    wait(act.at[: SPACE - 1], recv.at[7])
+    wait(act.at[:7], recv.at[12])
+    wait(mo_all.at[:128], recv.at[11])
 
     def rows_of(which):
-        blocks = act[pl.ds(16 * which, 16)]
-        lines = [jnp.concatenate([blocks[4 * band + lb] for lb in range(4)], axis=1) for band in range(4)]
-        return jnp.concatenate(lines, axis=0)
+        return act[pl.ds(4 * which, 4)].reshape(64, 512)
 
     po[...] = jnp.dot(rows_of(other), mo_all[...], preferred_element_type=F32)
     remote(po, pr, send.at[8], recv.at[8], partner)
@@ -289,14 +325,18 @@
         wait(rh.at[i], halo_send.at[3 + i])
         wait(rd.at[i], halo_send.at[5 + i])
     wait(w_ref, send.at[0])
-    wait(mi_all.at[:, :896], send.at[1])
-    wait(xall.at[:, :112], send.at[2])
-    wait(mo_all.at[:448], send.at[3])
+    wait(mi_all.at[:, :640], send.at[1])
+    wait(xall.at[:, :80], send.at[2])
+    wait(mo_all.at[:320], send.at[3])
     wait(st.at[:15], send.at[4])
     wait(eh.at[0], send.at[5])
-    wait(rs.at[: SPACE - 1], send.at[6])
-    wait(act.at[: SPACE - 1], send.at[7])
+    wait(rs.at[:7], send.at[6])
+    wait(quarter.at[:3], send.at[7])
     wait(po, send.at[8])
+    wait(xall.at[:, :32], send.at[9])
+    wait(mi_all.at[:, :256], send.at[10])
+    wait(mo_all.at[:128], send.at[11])
+    wait(act.at[:7], send.at[12])
 
 
 def shards(
@@ -321,7 +361,7 @@
     w = w.transpose(1, 3, 4, 2, 0, 5).reshape(512, 256)
     eb = jnp.pad(embed_bias.reshape(16, 64), ((0, 0), (64, 0)))
     mi = jnp.concatenate([mix_in[:512], mix_in[512:]], axis=1)
-    mb = mix_in_bias.reshape(8, 2, 64).transpose(1, 0, 2).reshape(2, 4, 128)
+    mb = mix_in_bias.reshape(8, 2, 64).transpose(1, 0, 2).reshape(2, 512)
     out = pl.pallas_call(
         kernel,
         out_shape=jax.ShapeDtypeStruct((64, 1024), BF16),
@@ -339,15 +379,16 @@
             pltpu.VMEM((16, 2, 512), F32),
             pltpu.VMEM((512, 1024), BF16),
             pltpu.VMEM((512, 1024), BF16),
-            pltpu.VMEM((SPACE, 16, 128), BF16),
-            pltpu.VMEM((SPACE, 16, 128), BF16),
-            pltpu.VMEM((SPACE, 16, 128), BF16),
+            pltpu.VMEM((8, 16, 512), BF16),
+            pltpu.VMEM((8, 16, 512), BF16),
+            pltpu.VMEM((4, 16, 512), BF16),
+            pltpu.VMEM((8, 16, 512), BF16),
             pltpu.VMEM((64, 1024), F32),
             pltpu.VMEM((64, 1024), F32),
             pltpu.SemaphoreType.DMA((7,)),
             pltpu.SemaphoreType.DMA((7,)),
-            pltpu.SemaphoreType.DMA((9,)),
-            pltpu.SemaphoreType.DMA((9,)),
+            pltpu.SemaphoreType.DMA((13,)),
+            pltpu.SemaphoreType.DMA((13,)),
             pltpu.SemaphoreType.DMA((3,)),
         ],
         compiler_params=pltpu.CompilerParams(collective_id=0, has_side_effects=True),

time: 86.4 us -> 75.7 us (0.88)
  Pallas kernels: 75.4 us -> 64.7 us
    pallas_call x1, Pallas kernels: 75.4 us -> 64.7 us  [shards(): pl.pallas_call(kernel, out_shape=jax.ShapeDtypeStruct((64, 1024), BF16),...]
where the time goes in v2:
time: 75.7 us; the launch traced here: 75.4 us
  Pallas kernels  64.7 us (85%)
  local copies, waits for them, and re-layouts  8.95 us (12%)
  other arithmetic  1.64 us (2%)
    pallas_call x1, Pallas kernels, shards(): pl.pallas_call(kernel, out_shape=jax.ShapeDtypeStruct((64, 1024), BF16),...  64.7 us
    unnamed x15, local copies, waits for them, and re-layouts  2.57 us

profile of v2, /device:TPU:1, one launch (start us, length us, event | category | flops | bytes accessed | tf_op | source)
XLA Modules:
  0.0 75.4 jit_solution(11421258448724022203)
XLA Ops:
  0.0 1.2 %copy.16 = bf16[20,8,4,32]{0,3,1,2:T(8,128)(2,1)S(1)} copy(bf16[20,8,4,32]{3,2,1,0:T(4,128)(2,1)} %bitcast.27) | data formatting | bytes 81920 | tf_op jit(solution)/shard_map/convert_element_type | solution.py:355
  1.2 0.3 reshape.36
  1.6 0.0 copy-start.2
  1.6 0.7 pad_convert_fusion.t1_ref
  2.3 0.1 copy-done.2
  2.4 0.1 pad_bitcast_fusion.3
  2.5 0.1 pad_maximum_fusion
  2.6 0.1 copy.17
  2.8 0.0 copy-start
  2.8 0.2 reshape.37
  3.0 0.6 pad.40
  3.6 0.0 copy-start.5
  3.6 0.7 copy-done.5
  4.3 0.6 broadcast_in_dim_tile.3.sb_ref
  4.9 0.0 copy-done
  4.9 0.1 pad.41
  5.0 0.5 copy.25
  5.5 0.0 copy-start.3
  5.5 0.0 copy-start.1
  5.5 1.0 %reshape.40.w_ref = bf16[512,256]{1,0:T(8,128)(2,1)} reshape(bf16[4,4,32,2,2,64]{5,4,3,2,1,0:T(2,128)(2,1)S(1)} %bitcast.23) | data formatting | bytes 524288 | tf_op jit(solution)/shard_map/reshape | solution.py:361
  6.6 0.0 copy-done.3
  6.6 0.1 reshape.41
  6.7 0.7 pad.42.eb_ref
  7.3 0.0 copy-done.1
  7.3 0.1 copy.23
  7.5 0.1 copy.22
  7.6 0.0 copy-start.4
  7.6 0.8 %pad_maximum_fusion.1.mi_ref = bf16[512,128]{1,0:T(8,128)(2,1)} fusion(bf16[512,64]{1,0:T(8,128)(2,1)S(1)} %copy.23, bf16[512,64]{1,0:T(8,128)(2,1)S(1)} %copy.22), kind=kLoop, calls=%fused_computation.2 | loop fusion | flops 262144 | bytes 262144 | tf_op jit(solution)/shard_map/concatenate | solution.py:363
  8.4 0.0 copy-done.4
  8.4 0.1 reshape.44
  8.5 0.7 reshape.45.mb_ref
  9.1 64.7 %shard_map.109 = bf16[64,1024]{1,0:T(8,128)(2,1)} custom-call(f32[32,896]{1,0:T(8,128)} %pad_convert_fusion.t1_ref, bf16[384,128]{1,0:T(8,128)(2,1)} %bitcast.26, f32[1,128]{1,0:T(1,128)} %broadcast_in_dim_tile.3.sb_ref, bf16[512,256]{1,0:T(8,128)(2,1)} %reshape.40.w_ref, f32[16,128]{1,0:T(8,128)} %pad.42.eb_ref, f32[8,128]{1,0:T(8,128)} %bitcast.29, ...), custom_call_target="tpu_custom_call" | custom-call | tf_op jit(solution)/shard_map/pallas_call | solution.py:365
  73.9 1.6 %copy.27 = bf16[1,64,1024]{2,1,0:T(8,128)(2,1)} copy(bf16[1,64,1024]{2,1,0:T(8,128)(2,1)} %bitcast.25) | data formatting | bytes 262144
  (3 shorter events, 0.0 us)
Async XLA Ops:
  1.6 0.8 %copy-start.2 = (bf16[3,3,20,32]{3,2,1,0:T(8,128)(2,1)S(1)}, bf16[3,3,20,32]{3,2,1,0:T(8,128)(2,1)}, u32[]{:S(2)}) copy-start(bf16[3,3,20,32]{3,2,1,0:T(8,128)(2,1)} %param.12) | copy-start | bytes 34564
  2.8 2.1 %copy-start = (bf16[7,7,32,64]{3,2,1,0:T(8,128)(2,1)S(1)}, bf16[7,7,32,64]{3,2,1,0:T(8,128)(2,1)}, u32[]{:S(2)}) copy-start(bf16[7,7,32,64]{3,2,1,0:T(8,128)(2,1)} %param.14) | copy-start | bytes 602116
  3.6 0.7 copy-start.5
  5.5 1.1 %copy-start.3 = (f32[1024]{0:T(1024)S(1)}, f32[1024]{0:T(1024)}, u32[]{:S(2)}) copy-start(f32[1024]{0:T(1024)} %param.15) | copy-start | bytes 12292
  5.5 1.8 %copy-start.1 = (bf16[1024,64]{0,1:T(8,128)(2,1)S(1)}, bf16[1024,64]{0,1:T(8,128)(2,1)}, u32[]{:S(2)}) copy-start(bf16[1024,64]{0,1:T(8,128)(2,1)} %param.18) | copy-start | bytes 393220
  7.6 0.8 %copy-start.4 = (f32[1024]{0:T(1024)S(1)}, f32[1024]{0:T(1024)}, u32[]{:S(2)}) copy-start(f32[1024]{0:T(1024)} %param.19) | copy-start | bytes 12292

commit v3 on v2

--- a/solution.py
+++ b/solution.py
@@ -20,18 +20,21 @@
 
 def kernel(
     t1_ref,
-    tw_ref,
+    stem_ref,
     sb_ref,
-    w_ref,
     eb_ref,
     gn_ref,
     nb_ref,
+    mb_ref,
+    ob_ref,
+    embed_ref,
     mi_ref,
-    mb_ref,
     mo_ref,
-    ob_ref,
     out_ref,
+    wide,
     aext,
+    taps,
+    filters,
     gc,
     rv,
     rh,
@@ -90,11 +93,35 @@
             passed = half(4 * r + ahead, 1)
             remote(passed, passed, ssem, rsem, chip(ring, behind))
 
-    def mi_half(owner, which):
-        return mi_all.at[256 * which : 256 * which + 256, pl.ds(pl.multiple_of(128 * owner, 128), 128)]
-
-    def mo_half(owner, which):
-        return mo_all.at[pl.ds(pl.multiple_of(64 * owner + 32 * which, 32), 32)]
+    def rows_from(buffer, owner, start, size):
+        return buffer.at[pl.ds(pl.multiple_of(64 * owner + start, 16), size)]
+
+    own_rows64 = pl.ds(pl.multiple_of(64 * k, 64), 64)
+
+    def first_round(mine, buffer, ssem, rsem):
+        for to in (chip(ring, ahead), chip(ring, behind), chip(1 - ring, x)):
+            remote(mine, buffer.at[own_rows64], ssem, rsem, to)
+
+    def second_round(buffer, ssem, rsem):
+        across, back, front = 4 * (1 - ring) + x, 4 * ring + behind, 4 * ring + ahead
+        for owner, start, to in (
+            (back, 0, chip(ring, ahead)),
+            (front, 32, chip(ring, behind)),
+            (across, 0, chip(ring, ahead)),
+            (across, 0, chip(ring, behind)),
+            (back, 32, chip(1 - ring, x)),
+            (front, 32, chip(1 - ring, x)),
+        ):
+            passed = rows_from(buffer, owner, start, 32)
+            remote(passed, passed, ssem, rsem, to)
+
+    def third_round(buffer, ssem, rsem):
+        passed = rows_from(buffer, 4 * ring + (x + 2) % 4, 32, 32)
+        remote(passed, passed, ssem, rsem, chip(1 - ring, x))
+        passed = rows_from(buffer, 4 * (1 - ring) + behind, 0, 16)
+        remote(passed, passed, ssem, rsem, chip(ring, ahead))
+        passed = rows_from(buffer, 4 * (1 - ring) + ahead, 16, 16)
+        remote(passed, passed, ssem, rsem, chip(ring, behind))
 
     def x_half(owner, which):
         return xall.at[:, pl.ds(pl.multiple_of(16 * owner, 16), 16), 256 * which : 256 * which + 256]
@@ -119,10 +146,20 @@
     greet(((2 * k + 15) % 16, side))
     greet(((2 * k + 2) % 16, side))
 
+    own_embed = pltpu.make_async_copy(embed_ref, filters, local.at[0])
+    own_embed.start()
+    own_mi = pltpu.make_async_copy(mi_ref, mi_all.at[own_rows64], local.at[1])
+    own_mi.start()
+    own_mo = pltpu.make_async_copy(mo_ref, mo_all.at[own_rows64], local.at[2])
+    own_mo.start()
+
+    wide[:, 0:128] = jnp.zeros((32, 128), F32)
+    wide[:, 128:768] = t1_ref[...].astype(F32)
+    wide[:, 768:1024] = jnp.zeros((32, 256), F32)
     for slot in range(10):
-        base = slot * 80 // 128 * 128
-        window = t1_ref[:, base : base + 256]
-        shift = slot * 80 - base
+        base = (28 + slot * 80) // 128 * 128
+        window = wide[:, base : base + 256]
+        shift = 28 + slot * 80 - base
         if shift:
             window = pltpu.roll(window, 256 - shift, axis=1)
         window = window[:, :128]
@@ -161,17 +198,33 @@
             halo_recv.at[5 + other],
             (2 * below + to, away),
         )
-    remote(w_ref, wall.at[core], send.at[0], recv.at[0], partner)
-    own_w = pltpu.make_async_copy(w_ref, wall.at[core], local.at[0])
-    own_w.start()
-    lanes_k = pl.ds(pl.multiple_of(128 * k, 128), 128)
-    own_mi = pltpu.make_async_copy(mi_ref, mi_all.at[:, lanes_k], local.at[1])
-    own_mi.start()
-    rows_k = pl.ds(pl.multiple_of(64 * k, 64), 64)
-    own_mo = pltpu.make_async_copy(mo_ref, mo_all.at[rows_k], local.at[2])
-    own_mo.start()
-
-    spread(mi_ref, mi_all.at[:, lanes_k], send.at[1], recv.at[1])
+    first_round(mi_ref, mi_all, send.at[1], recv.at[1])
+
+    spot = lax.broadcasted_iota(jnp.int32, (32, 128), 1)
+    repeat = (spot % 32 == lax.broadcasted_iota(jnp.int32, (32, 128), 0)).astype(BF16)
+    cell = lax.broadcasted_iota(jnp.int32, (20, 128), 1) // 32
+    taps[...] = jnp.zeros((384, 128), F32)
+    for row in range(3):
+        tiled = [jnp.dot(stem_ref[row, i], repeat, preferred_element_type=F32) for i in range(3)]
+        for column in range(6):
+            value = jnp.zeros((20, 128), F32)
+            for i in range(3):
+                if 0 <= column - i < 4:
+                    value = jnp.where(cell == column - i, tiled[i], value)
+            start = 128 * row + 20 * column
+            taps[start : start + 20] = value
+    stem_bias = jnp.concatenate([sb_ref[...]] * 4, axis=1)
+    own_embed.wait()
+    for row in range(4):
+        for column in range(4):
+            pieces = []
+            for b in range(2):
+                for a in range(2):
+                    i, j = 4 * a + row - 1, 4 * b + column - 1
+                    pieces.append(filters[i, j] if min(i, j) >= 0 else jnp.zeros((32, 64), BF16))
+            start = 32 * (4 * row + column)
+            wall[core, start : start + 32] = jnp.concatenate(pieces, axis=1)
+    remote(wall.at[core], wall.at[core], send.at[0], recv.at[0], partner)
 
     gc[:, :, own_rows] = aext[:, pl.ds(4 * core, 5)]
     wait(gc.at[:, :, own_rows], halo_recv.at[0])
@@ -207,9 +260,10 @@
     outside = jnp.logical_and(core == 0, s == 0)
     keep = jnp.logical_or(lax.broadcasted_iota(jnp.int32, (80, 128), 0) >= 16, jnp.logical_not(outside))
     rows16 = pl.ds(pl.multiple_of(16 * k, 16), 16)
+    tap = taps[...].astype(BF16)
     for row in range(4):
         patches = jnp.concatenate(lines[row : row + 3], axis=1)
-        stem = jnp.dot(patches, tw_ref[...], preferred_element_type=F32) + sb_ref[...]
+        stem = jnp.dot(patches, tap, preferred_element_type=F32) + stem_bias
         stem = jnp.where(keep, gelu(stem), 0.0)
         xall[:, rows16, 128 * row : 128 * row + 128] = stem.reshape(5, 16, 128).astype(BF16)
 
@@ -217,18 +271,20 @@
 
     wait(xall.at[:, :80], recv.at[2])
     forward(x_half, send.at[9], recv.at[9])
-    wait(mi_all.at[:, :640], recv.at[1])
-    forward(mi_half, send.at[10], recv.at[10])
-
-    own_w.wait()
-    wait(w_ref, recv.at[0])
+    wait(mi_all.at[:192], recv.at[1])
+    second_round(mi_all, send.at[10], recv.at[10])
+
+    wait(wall.at[0], recv.at[0])
     wait(xall.at[:, :32], recv.at[9])
     tokens = xall[...].reshape(640, 512)
+    low = lax.broadcasted_iota(jnp.int32, (1, 128), 1) < 64
+    bias_row = eb_ref[pl.ds(k, 1), :]
+    bias_rows = [jnp.where(low, 0.0, pltpu.roll(bias_row, 64, axis=1)), jnp.where(low, 0.0, bias_row)]
     lane = lax.broadcasted_iota(jnp.int32, (64, 128), 1)
     sums = [[0.0, 0.0] for _ in range(4)]
     for half in range(2):
         terms = jnp.dot(tokens, wall[half], preferred_element_type=F32)
-        both = terms[128:640, 128:256] + terms[0:512, 0:128] + eb_ref[pl.ds(2 * k + half, 1), :]
+        both = terms[128:640, 128:256] + terms[0:512, 0:128] + bias_rows[half]
         for column in range(4):
             turned = both[128 * column : 128 * column + 128].T
             shifted = pltpu.roll(turned[0:64], 1, axis=1)
@@ -247,13 +303,15 @@
 
     remote(eh.at[core], eh.at[core], send.at[5], recv.at[5], partner)
 
+    wait(mi_all.at[:192], recv.at[10])
+    third_round(mi_all, send.at[13], recv.at[13])
     gain = jnp.broadcast_to(gn_ref[pl.ds(k, 1), :], (128, 128)).T
     offset = jnp.broadcast_to(nb_ref[pl.ds(k, 1), :], (128, 128)).T
     gain = jnp.concatenate([gain] * 4, axis=1)
     offset = jnp.concatenate([offset] * 4, axis=1)
     wait(st.at[:15], recv.at[4])
     wait(eh.at[0], recv.at[5])
-    spread(mo_ref, mo_all.at[rows_k], send.at[3], recv.at[3])
+    first_round(mo_ref, mo_all, send.at[3], recv.at[3])
     normed = []
     for half in range(2):
         total = st[half]
@@ -264,24 +322,22 @@
         scale = lax.rsqrt(variance + 1e-05)
         value = (eh[half].astype(F32) - average) * scale * gain + offset
         normed.append(value.astype(BF16))
-    normed = jnp.concatenate(normed, axis=0)
+    normed = jnp.concatenate(normed, axis=1)
 
     own_mi.wait()
-    wait(mi_all.at[:, :256], recv.at[10])
-    low = lax.broadcasted_iota(jnp.int32, (128, 128), 1) < 64
-    for block in range(4):
-        prod = jnp.dot(normed, mi_all[:, 256 * block : 256 * block + 256], preferred_element_type=F32)
-        first = prod[0:128, 0:128] + pltpu.roll(prod[128:256, 0:128], 64, axis=1)
-        second = pltpu.roll(prod[0:128, 128:256], 64, axis=1) + prod[128:256, 128:256]
-        summed = jnp.where(low, first, second).astype(BF16)
-        for band in range(8):
-            hs[band, :, 128 * block : 128 * block + 128] = summed[16 * band : 16 * band + 16]
+    wait(mi_all.at[:64], recv.at[13])
+    summed = lax.dot_general(normed, mi_all[...], (((1,), (1,)), ((), ())), preferred_element_type=F32)
+    summed = summed.astype(BF16)
+    for band in range(8):
+        hs[band] = summed[16 * band : 16 * band + 16]
 
     @pl.loop(1, 8)
     def _(d):
         to = (z + d) % 8
         remote(hs.at[to], rs.at[z], send.at[6], recv.at[6], (c, 4 * to + part))
 
+    wait(mo_all.at[:192], recv.at[3])
+    second_round(mo_all, send.at[11], recv.at[11])
     rs[z] = hs[z]
     wait(rs.at[:7], recv.at[6])
     total = rs[0].astype(F32)
@@ -291,51 +347,64 @@
     for d in range(1, 4):
         to = 4 * z + (part + d) % 4
         remote(quarter.at[part], quarter.at[part], send.at[7], recv.at[7], (c, to))
-    wait(mo_all.at[:320], recv.at[3])
-    forward(mo_half, send.at[11], recv.at[11])
     wait(quarter.at[:3], recv.at[7])
     total = quarter[0].astype(F32)
     for source in range(1, 4):
         total = total + quarter[source].astype(F32)
-    total = total + mb_ref[pl.ds(core, 1), :]
+    rows = mb_ref[...]
+    turned = pltpu.roll(rows, 64, axis=1)
+    ours = jnp.where(low, jnp.where(core == 0, rows, turned), 0.0)
+    theirs = jnp.where(low, 0.0, jnp.where(core == 0, turned, rows))
+    hidden_bias = [ours[2 * i : 2 * i + 1] + theirs[2 * i + 1 : 2 * i + 2] for i in range(4)]
+    total = total + jnp.concatenate(hidden_bias, axis=1)
     act[z] = gelu(total).astype(BF16)
 
     @pl.loop(1, 8)
     def _(d):
         remote(act.at[z], act.at[z], send.at[12], recv.at[12], (c, (s + 4 * d) % SPACE))
 
+    wait(mo_all.at[:192], recv.at[11])
+    third_round(mo_all, send.at[14], recv.at[14])
     own_mo.wait()
     wait(act.at[:7], recv.at[12])
-    wait(mo_all.at[:128], recv.at[11])
+    wait(mo_all.at[:64], recv.at[14])
 
     def rows_of(which):
         return act[pl.ds(4 * which, 4)].reshape(64, 512)
 
-    po[...] = jnp.dot(rows_of(other), mo_all[...], preferred_element_type=F32)
-    remote(po, pr, send.at[8], recv.at[8], partner)
+    others = rows_of(other)
+    for half in range(2):
+        part_out = jnp.dot(others, mo_all[:, 512 * half : 512 * half + 512], preferred_element_type=F32)
+        po[half] = part_out
+        remote(po.at[half], pr.at[half], send.at[8 + 7 * half], recv.at[8 + 7 * half], partner)
     mine = jnp.dot(rows_of(core), mo_all[...], preferred_element_type=F32) + ob_ref[...]
     residual = [eh[half, pl.ds(pl.multiple_of(64 * core, 64), 64), :].astype(F32) for half in range(2)]
     mine = mine + jnp.concatenate(residual, axis=1)
-    wait(pr, recv.at[8])
-    out_ref[...] = (mine + pr[...]).astype(BF16)
+    for half in range(2):
+        wait(pr.at[half], recv.at[8 + 7 * half])
+        span = slice(512 * half, 512 * half + 512)
+        out_ref[:, span] = (mine[:, span] + pr[half]).astype(BF16)
 
     wait(gc.at[:, :, own_rows], halo_send.at[0])
     for i in range(2):
         wait(rv.at[i], halo_send.at[1 + i])
         wait(rh.at[i], halo_send.at[3 + i])
         wait(rd.at[i], halo_send.at[5 + i])
-    wait(w_ref, send.at[0])
-    wait(mi_all.at[:, :640], send.at[1])
+    wait(wall.at[0], send.at[0])
+    wait(mi_all.at[:192], send.at[1])
     wait(xall.at[:, :80], send.at[2])
-    wait(mo_all.at[:320], send.at[3])
+    wait(mo_all.at[:192], send.at[3])
     wait(st.at[:15], send.at[4])
     wait(eh.at[0], send.at[5])
     wait(rs.at[:7], send.at[6])
     wait(quarter.at[:3], send.at[7])
-    wait(po, send.at[8])
+    wait(po.at[0], send.at[8])
+    wait(po.at[1], send.at[15])
     wait(xall.at[:, :32], send.at[9])
-    wait(mi_all.at[:, :256], send.at[10])
-    wait(mo_all.at[:128], send.at[11])
+    wait(mi_all.at[:192], send.at[10])
+    wait(mo_all.at[:192], send.at[11])
+    wait(mi_all.at[:64], send.at[13])
+    wait(mo_all.at[:64], send.at[14])
     wait(act.at[:7], send.at[12])
 
 
@@ -352,23 +421,17 @@
     mix_out,
     mix_out_bias,
 ):
-    t1 = fields[0].astype(F32).reshape(20, 8, 4, 32).transpose(2, 1, 3, 0).reshape(32, 640)
-    t1 = jnp.pad(t1, ((0, 0), (100, 156)))
-    tw = jnp.stack([jnp.pad(stem_weight, ((0, 0), (i, 3 - i), (0, 0), (0, 0))) for i in range(4)], axis=3)
-    tw = jnp.pad(tw.reshape(3, 120, 128), ((0, 0), (0, 8), (0, 0))).reshape(384, 128)
-    sb = jnp.tile(stem_bias, 4)[None]
-    w = jnp.pad(embed_weight, ((1, 0), (1, 0), (0, 0), (0, 0))).reshape(2, 4, 2, 4, 32, 64)
-    w = w.transpose(1, 3, 4, 2, 0, 5).reshape(512, 256)
-    eb = jnp.pad(embed_bias.reshape(16, 64), ((0, 0), (64, 0)))
-    mi = jnp.concatenate([mix_in[:512], mix_in[512:]], axis=1)
-    mb = mix_in_bias.reshape(8, 2, 64).transpose(1, 0, 2).reshape(2, 512)
+    t1 = fields[0].reshape(20, 8, 4, 32).transpose(2, 1, 3, 0).reshape(32, 640)
     out = pl.pallas_call(
         kernel,
         out_shape=jax.ShapeDtypeStruct((64, 1024), BF16),
-        in_specs=[pl.BlockSpec(memory_space=pltpu.VMEM)] * 11,
+        in_specs=[pl.BlockSpec(memory_space=pltpu.VMEM)] * 8 + [pl.BlockSpec(memory_space=pl.ANY)] * 3,
         out_specs=pl.BlockSpec(memory_space=pltpu.VMEM),
         scratch_shapes=[
+            pltpu.VMEM((32, 1024), F32),
             pltpu.VMEM((4, 10, 8, 128), F32),
+            pltpu.VMEM((384, 128), F32),
+            pltpu.VMEM((7, 7, 32, 64), BF16),
             pltpu.VMEM((4, 5, 16, 128), F32),
             pltpu.VMEM((2, 5, 8, 128), F32),
             pltpu.VMEM((2, 4, 2, 8, 128), F32),
@@ -383,27 +446,27 @@
             pltpu.VMEM((8, 16, 512), BF16),
             pltpu.VMEM((4, 16, 512), BF16),
             pltpu.VMEM((8, 16, 512), BF16),
-            pltpu.VMEM((64, 1024), F32),
-            pltpu.VMEM((64, 1024), F32),
+            pltpu.VMEM((2, 64, 512), F32),
+            pltpu.VMEM((2, 64, 512), F32),
             pltpu.SemaphoreType.DMA((7,)),
             pltpu.SemaphoreType.DMA((7,)),
-            pltpu.SemaphoreType.DMA((13,)),
-            pltpu.SemaphoreType.DMA((13,)),
+            pltpu.SemaphoreType.DMA((16,)),
+            pltpu.SemaphoreType.DMA((16,)),
             pltpu.SemaphoreType.DMA((3,)),
         ],
         compiler_params=pltpu.CompilerParams(collective_id=0, has_side_effects=True),
     )(
         t1,
-        tw,
-        sb,
-        w,
-        eb,
+        stem_weight,
+        stem_bias[None],
+        embed_bias.reshape(8, 128),
         norm_gain.reshape(8, 128),
         norm_bias.reshape(8, 128),
-        mi,
-        mb,
+        mix_in_bias.reshape(8, 128),
+        mix_out_bias[None],
+        embed_weight,
+        mix_in.T,
         mix_out,
-        mix_out_bias[None],
     )
     return out[None]
 

time: 75.7 us -> 64 us (0.85)
  local copies, waits for them, and re-layouts: 8.95 us -> 3.78 us
  Pallas kernels: 64.7 us -> 60 us
  other arithmetic: 1.64 us -> 0 us
    pallas_call x1, Pallas kernels: 64.7 us -> 60 us  [shards(): pl.pallas_call(kernel, out_shape=jax.ShapeDtypeStruct((64, 1024), BF16),...]
    reshape x7 -> x1, local copies, waits for them, and re-layouts: 2.95 us -> 0.97 us  [shards(): t1 = fields[0].reshape(20, 8, 4, 32).transpose(2, 1, 3, 0).reshape(32, 640)]
    pad x3 -> x0, local copies, waits for them, and re-layouts: 1.41 us -> none  [the longest x1 0.67 us: shards(): eb = jnp.pad(embed_bias.reshape(16, 64), ((0, 0), (64, 0)))]
    convert_element_type x1 -> x0, local copies, waits for them, and re-layouts: 1.24 us -> none  [shards(): fields[0].astype(F32).reshape(20, 8, 4, 32).transpose(2, 1, 3, 0)]
    unnamed x15 -> x1, local copies, waits for them, and re-layouts: 2.57 us -> 1.57 us
    concatenate x1 -> x0, other arithmetic: 0.77 us -> none  [shards(): mi = jnp.concatenate([mix_in[:512], mix_in[512:]], axis=1)]
where the time goes in v3:
time: 64 us; the launch traced here: 63.8 us
  Pallas kernels  60 us (94%)
  local copies, waits for them, and re-layouts  3.78 us (6%)
    pallas_call x1, Pallas kernels, shards(): pl.pallas_call(kernel, out_shape=jax.ShapeDtypeStruct((64, 1024), BF16),...  60 us
    unnamed x1, local copies, waits for them, and re-layouts  1.57 us

profile of v3, /device:TPU:1, one launch (start us, length us, event | category | flops | bytes accessed | tf_op | source)
XLA Modules:
  0.0 63.8 jit_solution(1610568218171069759)
XLA Ops:
  0.0 1.2 %copy.13 = bf16[20,8,4,32]{0,3,1,2:T(8,128)(2,1)S(1)} copy(bf16[20,8,4,32]{3,2,1,0:T(4,128)(2,1)} %bitcast.14) | data formatting | bytes 81920 | tf_op jit(solution)/shard_map/reshape;squeeze | solution.py:424
  1.2 1.0 %reshape.15.t1_ref = bf16[32,640]{1,0:T(8,128)(2,1)} reshape(bf16[4,8,32,20]{3,2,1,0:T(8,128)(2,1)S(1)} %bitcast.12) | data formatting | bytes 81920 | tf_op jit(solution)/shard_map/reshape | solution.py:424
  2.2 60.0 %shard_map.109 = bf16[64,1024]{1,0:T(8,128)(2,1)} custom-call(bf16[32,640]{1,0:T(8,128)(2,1)} %reshape.15.t1_ref, bf16[3,3,20,32]{3,2,1,0:T(8,128)(2,1)} %stem_ref.1, f32[1,32]{1,0:T(1,128)} %bitcast.21, f32[8,128]{1,0:T(8,128)} %bitcast.16, f32[8,128]{1,0:T(8,128)} %bitcast.17, f32[8,128]{1,0:T(8,128)} %bitcast.18, f32[8,128]{1,0:T(8,128)} %bitcast.19, ...), custom_call_target="tpu_custom_call" | custom-call | tf_op jit(solution)/shard_map/pallas_call | solution.py:425
  62.3 1.6 %copy.15 = bf16[1,64,1024]{2,1,0:T(8,128)(2,1)} copy(bf16[1,64,1024]{2,1,0:T(8,128)(2,1)} %bitcast.13) | data formatting | bytes 262144

commit v4 on v3

--- a/solution.py
+++ b/solution.py
@@ -123,8 +123,18 @@
         passed = rows_from(buffer, 4 * (1 - ring) + ahead, 16, 16)
         remote(passed, passed, ssem, rsem, chip(ring, behind))
 
-    def x_half(owner, which):
-        return xall.at[:, pl.ds(pl.multiple_of(16 * owner, 16), 16), 256 * which : 256 * which + 256]
+    def x_half(slots, count, owner, which):
+        rows = pl.ds(pl.multiple_of(16 * owner, 16), 16)
+        return xall.at[pl.ds(slots, count), rows, 256 * which : 256 * which + 256]
+
+    def fetch(src, dst, index):
+        copy = pltpu.make_async_copy(src, dst, local.at[index])
+        copy.start()
+        return copy
+
+    own_embed = fetch(embed_ref, filters, 0)
+    own_mi = fetch(mi_ref, mi_all.at[own_rows64], 1)
+    own_mo = fetch(mo_ref, mo_all.at[own_rows64], 2)
 
     barrier = pltpu.get_barrier_semaphore()
 
@@ -145,13 +155,6 @@
     greet((2 * k + other, side))
     greet(((2 * k + 15) % 16, side))
     greet(((2 * k + 2) % 16, side))
-
-    own_embed = pltpu.make_async_copy(embed_ref, filters, local.at[0])
-    own_embed.start()
-    own_mi = pltpu.make_async_copy(mi_ref, mi_all.at[own_rows64], local.at[1])
-    own_mi.start()
-    own_mo = pltpu.make_async_copy(mo_ref, mo_all.at[own_rows64], local.at[2])
-    own_mo.start()
 
     wide[:, 0:128] = jnp.zeros((32, 128), F32)
     wide[:, 128:768] = t1_ref[...].astype(F32)
@@ -163,36 +166,29 @@
         if shift:
             window = pltpu.roll(window, 256 - shift, axis=1)
         window = window[:, :128]
-        for row in range(4):
-            aext[row, slot] = window[8 * row : 8 * row + 8]
+        aext[slot] = window.astype(BF16)
 
     pl.semaphore_wait(barrier, 29)
 
-    own_rows = pl.ds(pl.multiple_of(8 * core, 8), 8)
-    edge = 3 * core
+    edge = pl.ds(pl.multiple_of(16 * core, 16), 16)
     below = (k + 2 * core + CHIPS - 1) % CHIPS
-    remote(
-        aext.at[:, pl.ds(4 * other, 5)], gc.at[:, :, own_rows], halo_send.at[0], halo_recv.at[0], partner
-    )
+    remote(aext.at[pl.ds(4 * other, 5)], gc.at[:, core], halo_send.at[0], halo_recv.at[0], partner)
     for to in range(2):
         remote(
-            aext.at[edge, pl.ds(4 * to, 5)],
+            aext.at[pl.ds(4 * to, 5), edge],
             rv.at[other],
             halo_send.at[1 + to],
             halo_recv.at[1 + other],
             (2 * below + to, s),
         )
+    for to in range(2):
         away = right if to == 0 else left
-        start = 8 - 8 * to
+        side_slots = slice(8 - 8 * to, 10 - 8 * to)
         remote(
-            aext.at[:, start : start + 2],
-            rh.at[core],
-            halo_send.at[3 + to],
-            halo_recv.at[3 + core],
-            (2 * k + to, away),
+            aext.at[side_slots], rh.at[core], halo_send.at[3 + to], halo_recv.at[3 + core], (2 * k + to, away)
         )
         remote(
-            aext.at[edge, start : start + 2],
+            aext.at[side_slots, edge],
             rd.at[other],
             halo_send.at[5 + to],
             halo_recv.at[5 + other],
@@ -226,56 +222,70 @@
             wall[core, start : start + 32] = jnp.concatenate(pieces, axis=1)
     remote(wall.at[core], wall.at[core], send.at[0], recv.at[0], partner)
 
-    gc[:, :, own_rows] = aext[:, pl.ds(4 * core, 5)]
-    wait(gc.at[:, :, own_rows], halo_recv.at[0])
+    gc[:, core] = aext[pl.ds(4 * core, 5)]
+    at_left = jnp.logical_and(core == 0, s > 0)
+    at_right = jnp.logical_and(core == 1, s < SPACE - 1)
+    outside = jnp.logical_and(core == 0, s == 0)
+    rows16 = pl.ds(pl.multiple_of(16 * k, 16), 16)
+    tap = taps[...].astype(BF16)
+
+    def sides(ref, half, j):
+        first = jnp.where(at_left, ref[half, j].astype(F32), 0.0)
+        return first + jnp.where(at_right, ref[half, 0].astype(F32), 0.0) if j else first
+
+    def stem_of(slots, count, at_side):
+        height = 16 * count
+        blocks = [gc[slots + j, half].astype(F32) for j in range(count) for half in range(2)]
+        beyond = []
+        for half, inside in ((0, k > 0), (1, k < CHIPS - 1)):
+            slabs = []
+            for j in range(count):
+                value = rv[half, slots + j].astype(F32)
+                if at_side:
+                    value = value + sides(rd, half, j)
+                value = jnp.where(inside, value, 0.0)
+                value = value[15:16] if half == 0 else value[0:1]
+                slabs.append(jnp.broadcast_to(value, (16, 128)))
+            beyond.append(jnp.concatenate(slabs, axis=0))
+        if at_side:
+            blocks = [block + sides(rh, i % 2, i // 2) for i, block in enumerate(blocks)]
+        grid = [jnp.concatenate([block[8 * row : 8 * row + 8] for block in blocks], axis=0) for row in range(4)]
+        index = lax.broadcasted_iota(jnp.int32, (height, 128), 0)
+        before = jnp.where(index % 16 == 0, beyond[0], pltpu.roll(grid[3], 1, axis=0))
+        after = jnp.where(index % 16 == 15, beyond[1], pltpu.roll(grid[0], height - 1, axis=0))
+        lines = [line.astype(BF16) for line in (before, *grid, after)]
+        for row in range(4):
+            patches = jnp.concatenate(lines[row : row + 3], axis=1)
+            stem = gelu(jnp.dot(patches, tap, preferred_element_type=F32) + stem_bias)
+            if at_side:
+                stem = jnp.where(jnp.logical_or(index >= 16, jnp.logical_not(outside)), stem, 0.0)
+            stem = stem.reshape(count, 16, 128).astype(BF16)
+            xall[pl.ds(slots, count), rows16, 128 * row : 128 * row + 128] = stem
+        mine = xall.at[pl.ds(slots, count), rows16]
+        return mine
+
+    inner, outer = 2 - 2 * core, 3 * core
+    wait(gc.at[:, core], halo_recv.at[0])
     for i in range(2):
         wait(rv.at[i], halo_recv.at[1 + i])
+    mine = stem_of(inner, 3, False)
+    spread(mine, mine, send.at[2], recv.at[2])
+    for i in range(2):
         wait(rh.at[i], halo_recv.at[3 + i])
         wait(rd.at[i], halo_recv.at[5 + i])
-    at_left = jnp.logical_and(core == 0, s > 0)
-    at_right = jnp.logical_and(core == 1, s < SPACE - 1)
-    for half in range(2):
-        rows = slice(8 * half, 8 * half + 8)
-        for row in range(4):
-            for slot, use, column in ((0, at_left, 0), (1, at_left, 1), (4, at_right, 0)):
-                gc[row, slot, rows] += jnp.where(use, rh[half, row, column], 0.0)
-    beyond = []
-    for half, inside in ((0, k > 0), (1, k < CHIPS - 1)):
-        slabs = []
-        for slot in range(5):
-            value = rv[half, slot]
-            if slot in (0, 1):
-                value = value + jnp.where(at_left, rd[half, slot], 0.0)
-            if slot == 4:
-                value = value + jnp.where(at_right, rd[half, 0], 0.0)
-            value = jnp.where(inside, value, 0.0)
-            value = value[7:8] if half == 0 else value[0:1]
-            slabs.append(jnp.broadcast_to(value, (16, 128)))
-        beyond.append(jnp.concatenate(slabs, axis=0))
-    grid = [gc[row].reshape(80, 128) for row in range(4)]
-    place = lax.broadcasted_iota(jnp.int32, (80, 128), 0) % 16
-    before = jnp.where(place == 0, beyond[0], pltpu.roll(grid[3], 1, axis=0))
-    after = jnp.where(place == 15, beyond[1], pltpu.roll(grid[0], 79, axis=0))
-    lines = [line.astype(BF16) for line in (before, *grid, after)]
-    outside = jnp.logical_and(core == 0, s == 0)
-    keep = jnp.logical_or(lax.broadcasted_iota(jnp.int32, (80, 128), 0) >= 16, jnp.logical_not(outside))
-    rows16 = pl.ds(pl.multiple_of(16 * k, 16), 16)
-    tap = taps[...].astype(BF16)
-    for row in range(4):
-        patches = jnp.concatenate(lines[row : row + 3], axis=1)
-        stem = jnp.dot(patches, tap, preferred_element_type=F32) + stem_bias
-        stem = jnp.where(keep, gelu(stem), 0.0)
-        xall[:, rows16, 128 * row : 128 * row + 128] = stem.reshape(5, 16, 128).astype(BF16)
-
-    spread(xall.at[:, rows16], xall.at[:, rows16], send.at[2], recv.at[2])
-
-    wait(xall.at[:, :80], recv.at[2])
-    forward(x_half, send.at[9], recv.at[9])
+    mine = stem_of(outer, 2, True)
+    spread(mine, mine, send.at[16], recv.at[16])
+
+    wait(xall.at[:3, :80], recv.at[2])
+    forward(functools.partial(x_half, inner, 3), send.at[9], recv.at[9])
+    wait(xall.at[:2, :80], recv.at[16])
+    forward(functools.partial(x_half, outer, 2), send.at[17], recv.at[17])
     wait(mi_all.at[:192], recv.at[1])
     second_round(mi_all, send.at[10], recv.at[10])
 
     wait(wall.at[0], recv.at[0])
-    wait(xall.at[:, :32], recv.at[9])
+    wait(xall.at[:3, :32], recv.at[9])
+    wait(xall.at[:2, :32], recv.at[17])
     tokens = xall[...].reshape(640, 512)
     low = lax.broadcasted_iota(jnp.int32, (1, 128), 1) < 64
     bias_row = eb_ref[pl.ds(k, 1), :]
@@ -375,7 +385,7 @@
     others = rows_of(other)
     for half in range(2):
         part_out = jnp.dot(others, mo_all[:, 512 * half : 512 * half + 512], preferred_element_type=F32)
-        po[half] = part_out
+        po[half] = part_out.astype(BF16)
         remote(po.at[half], pr.at[half], send.at[8 + 7 * half], recv.at[8 + 7 * half], partner)
     mine = jnp.dot(rows_of(core), mo_all[...], preferred_element_type=F32) + ob_ref[...]
     residual = [eh[half, pl.ds(pl.multiple_of(64 * core, 64), 64), :].astype(F32) for half in range(2)]
@@ -383,16 +393,17 @@
     for half in range(2):
         wait(pr.at[half], recv.at[8 + 7 * half])
         span = slice(512 * half, 512 * half + 512)
-        out_ref[:, span] = (mine[:, span] + pr[half]).astype(BF16)
-
-    wait(gc.at[:, :, own_rows], halo_send.at[0])
+        out_ref[:, span] = (mine[:, span] + pr[half].astype(F32)).astype(BF16)
+
+    wait(gc.at[:, core], halo_send.at[0])
     for i in range(2):
         wait(rv.at[i], halo_send.at[1 + i])
         wait(rh.at[i], halo_send.at[3 + i])
         wait(rd.at[i], halo_send.at[5 + i])
     wait(wall.at[0], send.at[0])
     wait(mi_all.at[:192], send.at[1])
-    wait(xall.at[:, :80], send.at[2])
+    wait(xall.at[:3, :80], send.at[2])
+    wait(xall.at[:2, :80], send.at[16])
     wait(mo_all.at[:192], send.at[3])
     wait(st.at[:15], send.at[4])
     wait(eh.at[0], send.at[5])
@@ -400,7 +411,8 @@
     wait(quarter.at[:3], send.at[7])
     wait(po.at[0], send.at[8])
     wait(po.at[1], send.at[15])
-    wait(xall.at[:, :32], send.at[9])
+    wait(xall.at[:3, :32], send.at[9])
+    wait(xall.at[:2, :32], send.at[17])
     wait(mi_all.at[:192], send.at[10])
     wait(mo_all.at[:192], send.at[11])
     wait(mi_all.at[:64], send.at[13])
@@ -425,17 +437,17 @@
     out = pl.pallas_call(
         kernel,
         out_shape=jax.ShapeDtypeStruct((64, 1024), BF16),
-        in_specs=[pl.BlockSpec(memory_space=pltpu.VMEM)] * 8 + [pl.BlockSpec(memory_space=pl.ANY)] * 3,
+        in_specs=[pl.BlockSpec(memory_space=pltpu.VMEM)] * 8 + [pl.BlockSpec(memory_space=pltpu.HBM)] * 3,
         out_specs=pl.BlockSpec(memory_space=pltpu.VMEM),
         scratch_shapes=[
             pltpu.VMEM((32, 1024), F32),
-            pltpu.VMEM((4, 10, 8, 128), F32),
+            pltpu.VMEM((10, 32, 128), BF16),
             pltpu.VMEM((384, 128), F32),
             pltpu.VMEM((7, 7, 32, 64), BF16),
-            pltpu.VMEM((4, 5, 16, 128), F32),
-            pltpu.VMEM((2, 5, 8, 128), F32),
-            pltpu.VMEM((2, 4, 2, 8, 128), F32),
-            pltpu.VMEM((2, 2, 8, 128), F32),
+            pltpu.VMEM((5, 2, 32, 128), BF16),
+            pltpu.VMEM((2, 5, 16, 128), BF16),
+            pltpu.VMEM((2, 2, 32, 128), BF16),
+            pltpu.VMEM((2, 2, 16, 128), BF16),
             pltpu.VMEM((5, 128, 512), BF16),
             pltpu.VMEM((2, 512, 256), BF16),
             pltpu.VMEM((2, 128, 512), BF16),
@@ -446,15 +458,15 @@
             pltpu.VMEM((8, 16, 512), BF16),
             pltpu.VMEM((4, 16, 512), BF16),
             pltpu.VMEM((8, 16, 512), BF16),
-            pltpu.VMEM((2, 64, 512), F32),
-            pltpu.VMEM((2, 64, 512), F32),
+            pltpu.VMEM((2, 64, 512), BF16),
+            pltpu.VMEM((2, 64, 512), BF16),
             pltpu.SemaphoreType.DMA((7,)),
             pltpu.SemaphoreType.DMA((7,)),
-            pltpu.SemaphoreType.DMA((16,)),
-            pltpu.SemaphoreType.DMA((16,)),
+            pltpu.SemaphoreType.DMA((18,)),
+            pltpu.SemaphoreType.DMA((18,)),
             pltpu.SemaphoreType.DMA((3,)),
         ],
-        compiler_params=pltpu.CompilerParams(collective_id=0, has_side_effects=True),
+        compiler_params=pltpu.CompilerParams(collective_id=0, has_side_effects=True, vmem_limit_bytes=16 * 2**20),
     )(
         t1,
         stem_weight,

time: 64 us -> 60.3 us (0.942)
  Pallas kernels: 60 us -> 57.2 us
  local copies, waits for them, and re-layouts: 3.78 us -> 2.87 us
    pallas_call x1, Pallas kernels: 60 us -> 57.2 us  [shards(): pl.pallas_call(kernel, out_shape=jax.ShapeDtypeStruct((64, 1024), BF16),...]
    unnamed x1 -> x21, local copies, waits for them, and re-layouts: 1.57 us -> 1.23 us
where the time goes in v4:
time: 60.3 us; the launch traced here: 60.1 us
  Pallas kernels  57.2 us (95%)
  local copies, waits for them, and re-layouts  2.87 us (5%)
    pallas_call x1, Pallas kernels, shards(): pl.pallas_call(kernel, out_shape=jax.ShapeDtypeStruct((64, 1024), BF16),...  57.2 us
    another operation x1, local copies, waits for them, and re-layouts, shards(): t1 = fields[0].reshape(20, 8, 4, 32).transpose(2, 1, 3, 0).reshape(32, 640)  1.29 us
    unnamed x21, local copies, waits for them, and re-layouts  1.23 us

profile of v4, /device:TPU:1, one launch (start us, length us, event | category | flops | bytes accessed | tf_op | source)
XLA Modules:
  0.0 60.1 jit_solution(14256820684028823027)
XLA Ops:
  0.0 0.0 copy-start
  0.0 0.0 copy-start.3
  0.0 1.3 %copy.13 = bf16[20,8,4,32]{0,3,1,2:T(8,128)(2,1)S(1)} copy(bf16[20,8,4,32]{3,2,1,0:T(4,128)(2,1)} %bitcast.21) | data formatting | bytes 81920 | tf_op jit(solution)/shard_map/reshape;squeeze | solution.py:436
  1.3 0.0 copy-start.1
  1.3 0.0 copy-start.2
  1.3 0.0 copy-start.4
  1.3 0.0 copy-start.5
  1.3 0.0 copy-start.6
  1.4 0.0 copy-start.7
  1.4 0.0 copy-start.8
  1.4 0.0 copy-start.9
  1.4 0.3 reshape.15.t1_ref
  1.7 0.0 copy-done
  1.7 0.0 copy-done.3
  1.7 0.5 copy-done.1
  2.2 0.1 copy-done.2
  2.3 0.0 copy-done.4
  2.3 0.0 copy-done.5
  2.3 0.0 copy-done.6
  2.3 0.0 copy-done.7
  2.3 0.0 copy-done.8
  2.3 0.0 copy-done.9
  2.3 57.2 %shard_map.109 = bf16[64,1024]{1,0:T(8,128)(2,1)S(1)} custom-call(bf16[32,640]{1,0:T(8,128)(2,1)S(1)} %reshape.15.t1_ref, bf16[3,3,20,32]{3,2,1,0:T(8,128)(2,1)S(1)} %copy-done.3, f32[1,32]{1,0:T(1,128)S(1)} %bitcast.19, f32[8,128]{1,0:T(8,128)S(1)} %bitcast.14, f32[8,128]{1,0:T(8,128)S(1)} %bitcast.15, f32[8,128]{1,0:T(8,128)S(1)} %bitcast.16, ...), custom_call_target="tpu_custom_call" | custom-call | tf_op jit(solution)/shard_map/pallas_call | solution.py:437
  59.5 0.7 %copy.15 = bf16[1,64,1024]{2,1,0:T(8,128)(2,1)} copy(bf16[1,64,1024]{2,1,0:T(8,128)(2,1)S(1)} %bitcast.12) | data formatting | bytes 262144
Async XLA Ops:
  0.0 1.7 %copy-start = (bf16[7,7,32,64]{3,2,1,0:T(8,128)(2,1)S(1)}, bf16[7,7,32,64]{3,2,1,0:T(8,128)(2,1)}, u32[]{:S(2)}) copy-start(bf16[7,7,32,64]{3,2,1,0:T(8,128)(2,1)} %embed_ref.1) | copy-start | bytes 602116
  0.0 1.7 %copy-start.3 = (bf16[3,3,20,32]{3,2,1,0:T(8,128)(2,1)S(1)}, bf16[3,3,20,32]{3,2,1,0:T(8,128)(2,1)}, u32[]{:S(2)}) copy-start(bf16[3,3,20,32]{3,2,1,0:T(8,128)(2,1)} %stem_ref.1) | copy-start | bytes 34564
  1.3 0.9 %copy-start.1 = (bf16[1024,64]{0,1:T(8,128)(2,1)S(1)}, bf16[1024,64]{0,1:T(8,128)(2,1)}, u32[]{:S(2)}) copy-start(bf16[1024,64]{0,1:T(8,128)(2,1)} %param.18) | copy-start | bytes 393220
  1.3 1.0 %copy-start.2 = (bf16[64,1024]{1,0:T(8,128)(2,1)S(1)}, bf16[64,1024]{1,0:T(8,128)(2,1)}, u32[]{:S(2)}) copy-start(bf16[64,1024]{1,0:T(8,128)(2,1)} %mo_ref.1) | copy-start | bytes 393220
  1.3 1.0 %copy-start.4 = (f32[1024]{0:T(1024)S(1)}, f32[1024]{0:T(1024)}, u32[]{:S(2)}) copy-start(f32[1024]{0:T(1024)} %param.15) | copy-start | bytes 12292
  1.3 0.9 %copy-start.5 = (f32[1024]{0:T(1024)S(1)}, f32[1024]{0:T(1024)}, u32[]{:S(2)}) copy-start(f32[1024]{0:T(1024)} %param.16) | copy-start | bytes 12292
  1.3 0.9 %copy-start.6 = (f32[1024]{0:T(1024)S(1)}, f32[1024]{0:T(1024)}, u32[]{:S(2)}) copy-start(f32[1024]{0:T(1024)} %param.17) | copy-start | bytes 12292
  1.4 0.9 %copy-start.7 = (f32[1024]{0:T(1024)S(1)}, f32[1024]{0:T(1024)}, u32[]{:S(2)}) copy-start(f32[1024]{0:T(1024)} %param.19) | copy-start | bytes 12292
  1.4 0.9 %copy-start.8 = (f32[1024]{0:T(1024)S(1)}, f32[1024]{0:T(1024)}, u32[]{:S(2)}) copy-start(f32[1024]{0:T(1024)} %param.21) | copy-start | bytes 12292
  1.4 0.9 %copy-start.9 = (f32[32]{0:T(128)S(1)}, f32[32]{0:T(128)}, u32[]{:S(2)}) copy-start(f32[32]{0:T(128)} %param.13) | copy-start | bytes 388

commit v5 on v4

--- a/solution.py
+++ b/solution.py
@@ -19,7 +19,20 @@
 
 
 def kernel(
-    t1_ref,
+    stem_in,
+    sb_in,
+    eb_in,
+    gn_in,
+    nb_in,
+    mb_in,
+    ob_in,
+    filters_in,
+    fields_ref,
+    mi_ref,
+    mo_ref,
+    out_ref,
+    cells,
+    filters,
     stem_ref,
     sb_ref,
     eb_ref,
@@ -27,14 +40,8 @@
     nb_ref,
     mb_ref,
     ob_ref,
-    embed_ref,
-    mi_ref,
-    mo_ref,
-    out_ref,
-    wide,
     aext,
     taps,
-    filters,
     gc,
     rv,
     rh,
@@ -102,17 +109,16 @@
         for to in (chip(ring, ahead), chip(ring, behind), chip(1 - ring, x)):
             remote(mine, buffer.at[own_rows64], ssem, rsem, to)
 
-    def second_round(buffer, ssem, rsem):
+    def second_round(buffer, ssem, rsem, along):
         across, back, front = 4 * (1 - ring) + x, 4 * ring + behind, 4 * ring + ahead
-        for owner, start, to in (
-            (back, 0, chip(ring, ahead)),
-            (front, 32, chip(ring, behind)),
-            (across, 0, chip(ring, ahead)),
-            (across, 0, chip(ring, behind)),
-            (back, 32, chip(1 - ring, x)),
-            (front, 32, chip(1 - ring, x)),
-        ):
-            passed = rows_from(buffer, owner, start, 32)
+        hops = [(back, 0, 32, chip(ring, ahead)), (front, 32, 32, chip(ring, behind))]
+        if along:
+            hops += [(across, 0, 64, chip(ring, ahead)), (across, 0, 64, chip(ring, behind))]
+        else:
+            hops += [(across, 0, 32, chip(ring, ahead)), (across, 0, 32, chip(ring, behind))]
+            hops += [(back, 32, 32, chip(1 - ring, x)), (front, 32, 32, chip(1 - ring, x))]
+        for owner, start, size, to in hops:
+            passed = rows_from(buffer, owner, start, size)
             remote(passed, passed, ssem, rsem, to)
 
     def third_round(buffer, ssem, rsem):
@@ -132,10 +138,7 @@
         copy.start()
         return copy
 
-    own_embed = fetch(embed_ref, filters, 0)
-    own_mi = fetch(mi_ref, mi_all.at[own_rows64], 1)
-    own_mo = fetch(mo_ref, mo_all.at[own_rows64], 2)
-
+    own_fields = fetch(fields_ref, cells, 0)
     barrier = pltpu.get_barrier_semaphore()
 
     def greet(to):
@@ -156,17 +159,26 @@
     greet(((2 * k + 15) % 16, side))
     greet(((2 * k + 2) % 16, side))
 
-    wide[:, 0:128] = jnp.zeros((32, 128), F32)
-    wide[:, 128:768] = t1_ref[...].astype(F32)
-    wide[:, 768:1024] = jnp.zeros((32, 256), F32)
-    for slot in range(10):
-        base = (28 + slot * 80) // 128 * 128
-        window = wide[:, base : base + 256]
-        shift = 28 + slot * 80 - base
-        if shift:
-            window = pltpu.roll(window, 256 - shift, axis=1)
-        window = window[:, :128]
-        aext[slot] = window.astype(BF16)
+    own_filters = fetch(filters_in, filters, 1)
+    own_stem = fetch(stem_in, stem_ref, 2)
+    own_mi = fetch(mi_ref, mi_all.at[own_rows64], 3)
+    own_mo = fetch(mo_ref, mo_all.at[own_rows64], 4)
+    rest = [(sb_in, sb_ref), (eb_in, eb_ref), (gn_in, gn_ref), (nb_in, nb_ref), (mb_in, mb_ref), (ob_in, ob_ref)]
+    own_rest = [fetch(src, dst, 5 + i) for i, (src, dst) in enumerate(rest)]
+
+    source = lax.broadcasted_iota(jnp.int32, (640, 256), 0)
+    target = lax.broadcasted_iota(jnp.int32, (640, 256), 1)
+    target = target % 128 + target // 128 * 80 - (source % 32 + 5) * 20 - source // 32
+    order = lax.broadcasted_iota(jnp.int32, (32, 32), 0)
+    order = 4 * (order % 8) + order // 8 == lax.broadcasted_iota(jnp.int32, (32, 32), 1)
+    own_fields.wait()
+    grid = jnp.concatenate([cells[i] for i in range(20)], axis=1)
+    grid = jnp.dot(order.astype(BF16), grid, preferred_element_type=F32).astype(BF16)
+    for pair in range(5):
+        chosen = (target == -160 * pair).astype(BF16)
+        window = jnp.dot(grid, chosen, preferred_element_type=F32).astype(BF16)
+        aext[2 * pair] = window[:, :128]
+        aext[2 * pair + 1] = window[:, 128:]
 
     pl.semaphore_wait(barrier, 29)
 
@@ -199,6 +211,9 @@
     spot = lax.broadcasted_iota(jnp.int32, (32, 128), 1)
     repeat = (spot % 32 == lax.broadcasted_iota(jnp.int32, (32, 128), 0)).astype(BF16)
     cell = lax.broadcasted_iota(jnp.int32, (20, 128), 1) // 32
+    own_stem.wait()
+    for copy in own_rest:
+        copy.wait()
     taps[...] = jnp.zeros((384, 128), F32)
     for row in range(3):
         tiled = [jnp.dot(stem_ref[row, i], repeat, preferred_element_type=F32) for i in range(3)]
@@ -210,7 +225,7 @@
             start = 128 * row + 20 * column
             taps[start : start + 20] = value
     stem_bias = jnp.concatenate([sb_ref[...]] * 4, axis=1)
-    own_embed.wait()
+    own_filters.wait()
     for row in range(4):
         for column in range(4):
             pieces = []
@@ -281,7 +296,7 @@
     wait(xall.at[:2, :80], recv.at[16])
     forward(functools.partial(x_half, outer, 2), send.at[17], recv.at[17])
     wait(mi_all.at[:192], recv.at[1])
-    second_round(mi_all, send.at[10], recv.at[10])
+    second_round(mi_all, send.at[10], recv.at[10], False)
 
     wait(wall.at[0], recv.at[0])
     wait(xall.at[:3, :32], recv.at[9])
@@ -347,7 +362,7 @@
         remote(hs.at[to], rs.at[z], send.at[6], recv.at[6], (c, 4 * to + part))
 
     wait(mo_all.at[:192], recv.at[3])
-    second_round(mo_all, send.at[11], recv.at[11])
+    second_round(mo_all, send.at[11], recv.at[11], True)
     rs[z] = hs[z]
     wait(rs.at[:7], recv.at[6])
     total = rs[0].astype(F32)
@@ -433,17 +448,23 @@
     mix_out,
     mix_out_bias,
 ):
-    t1 = fields[0].reshape(20, 8, 4, 32).transpose(2, 1, 3, 0).reshape(32, 640)
     out = pl.pallas_call(
         kernel,
-        out_shape=jax.ShapeDtypeStruct((64, 1024), BF16),
-        in_specs=[pl.BlockSpec(memory_space=pltpu.VMEM)] * 8 + [pl.BlockSpec(memory_space=pltpu.HBM)] * 3,
+        out_shape=pltpu.VMEM((64, 1024), BF16),
+        in_specs=[pl.BlockSpec(memory_space=pl.ANY)] * 11,
         out_specs=pl.BlockSpec(memory_space=pltpu.VMEM),
         scratch_shapes=[
-            pltpu.VMEM((32, 1024), F32),
+            pltpu.VMEM((20, 32, 32), BF16),
+            pltpu.VMEM((7, 7, 32, 64), BF16),
+            pltpu.VMEM((3, 3, 20, 32), BF16),
+            pltpu.VMEM((1, 32), F32),
+            pltpu.VMEM((8, 128), F32),
+            pltpu.VMEM((8, 128), F32),
+            pltpu.VMEM((8, 128), F32),
+            pltpu.VMEM((8, 128), F32),
+            pltpu.VMEM((1, 1024), F32),
             pltpu.VMEM((10, 32, 128), BF16),
             pltpu.VMEM((384, 128), F32),
-            pltpu.VMEM((7, 7, 32, 64), BF16),
             pltpu.VMEM((5, 2, 32, 128), BF16),
             pltpu.VMEM((2, 5, 16, 128), BF16),
             pltpu.VMEM((2, 2, 32, 128), BF16),
@@ -464,11 +485,10 @@
             pltpu.SemaphoreType.DMA((7,)),
             pltpu.SemaphoreType.DMA((18,)),
             pltpu.SemaphoreType.DMA((18,)),
-            pltpu.SemaphoreType.DMA((3,)),
+            pltpu.SemaphoreType.DMA((11,)),
         ],
-        compiler_params=pltpu.CompilerParams(collective_id=0, has_side_effects=True, vmem_limit_bytes=16 * 2**20),
+        compiler_params=pltpu.CompilerParams(collective_id=0, has_side_effects=True, vmem_limit_bytes=58 * 2**20),
     )(
-        t1,
         stem_weight,
         stem_bias[None],
         embed_bias.reshape(8, 128),
@@ -477,6 +497,7 @@
         mix_in_bias.reshape(8, 128),
         mix_out_bias[None],
         embed_weight,
+        fields[0],
         mix_in.T,
         mix_out,
     )

time: 60.3 us -> 56.2 us (0.932)
  local copies, waits for them, and re-layouts: 2.87 us -> 0.66 us
  Pallas kernels: 57.2 us -> 55.4 us
    pallas_call x1, Pallas kernels: 57.2 us -> 55.4 us  [shards(): pl.pallas_call(kernel, out_shape=pltpu.VMEM((64, 1024), BF16), in_specs=[...]
    another operation x1 -> x0, local copies, waits for them, and re-layouts: 1.29 us -> none  [shards(): t1 = fields[0].reshape(20, 8, 4, 32).transpose(2, 1, 3, 0).reshape(32, 640)]
    unnamed x21 -> x1, local copies, waits for them, and re-layouts: 1.23 us -> 0.66 us
where the time goes in v5:
time: 56.2 us; the launch traced here: 56.1 us
  Pallas kernels  55.4 us (99%)
  local copies, waits for them, and re-layouts  0.66 us (1%)
    pallas_call x1, Pallas kernels, shards(): pl.pallas_call(kernel, out_shape=pltpu.VMEM((64, 1024), BF16), in_specs=[...  55.4 us

profile of v5, /device:TPU:1, one launch (start us, length us, event | category | flops | bytes accessed | tf_op | source)
XLA Modules:
  0.0 56.1 jit_solution(10792935090991080585)
XLA Ops:
  0.0 55.4 %shard_map.109 = bf16[64,1024]{1,0:T(8,128)(2,1)S(1)} custom-call(bf16[3,3,20,32]{3,2,1,0:T(8,128)(2,1)} %stem_in.1, f32[1,32]{1,0:T(1,128)} %bitcast.17, f32[8,128]{1,0:T(8,128)} %bitcast.12, f32[8,128]{1,0:T(8,128)} %bitcast.13, f32[8,128]{1,0:T(8,128)} %bitcast.14, f32[8,128]{1,0:T(8,128)} %bitcast.15, f32[1,1024]{1,0:T(1,128)} %bitcast.16, ...), custom_call_target="tpu_custom_call" | custom-call | tf_op jit(solution)/shard_map/pallas_call | solution.py:451
  55.4 0.7 %copy.13 = bf16[1,64,1024]{2,1,0:T(8,128)(2,1)} copy(bf16[1,64,1024]{2,1,0:T(8,128)(2,1)S(1)} %bitcast.9) | data formatting | bytes 262144

commit v6 on v5

--- a/solution.py
+++ b/solution.py
@@ -63,6 +63,7 @@
     send,
     recv,
     local,
+    meet,
 ):
     c, s = lax.axis_index("chan"), lax.axis_index("space")
     k, core = c // 2, c % 2
@@ -89,8 +90,10 @@
 
     near = [chip(ring, ahead), chip(ring, behind), chip(1 - ring, x), chip(1 - ring, ahead), chip(1 - ring, behind)]
 
-    def spread(src, dst, ssem, rsem):
-        for to in near:
+    far = [chip(1 - ring, (x + 2) % 4), chip(ring, (x + 2) % 4)]
+
+    def spread(src, dst, ssem, rsem, everyone=False):
+        for to in far + near[::-1] if everyone else near:
             remote(src, dst, ssem, rsem, to)
 
     def forward(half, ssem, rsem):
@@ -148,12 +151,16 @@
     def _(d):
         greet(((c + d) % 16, s))
 
-    @pl.loop(1, 8)
-    def _(d):
-        greet((c, (s + 4 * d) % SPACE))
-
-    for d in range(1, 4):
-        greet((c, 4 * z + (part + d) % 4))
+    def over_z(d):
+        return (c, (s + 4 * d) % SPACE)
+
+    def over_parts(d):
+        return (c, 4 * z + (part + d) % 4)
+
+    for d in (1, 7):
+        greet(over_z(d))
+    for d in (1, 3):
+        greet(over_parts(d))
     greet((c, side))
     greet((2 * k + other, side))
     greet(((2 * k + 15) % 16, side))
@@ -180,32 +187,58 @@
         aext[2 * pair] = window[:, :128]
         aext[2 * pair + 1] = window[:, 128:]
 
-    pl.semaphore_wait(barrier, 29)
+    pl.semaphore_wait(barrier, 23)
+
+    def tell(index, to):
+        pl.semaphore_signal(meet.at[index], inc=1, device_id=to, device_id_type=MESH)
+
 
     edge = pl.ds(pl.multiple_of(16 * core, 16), 16)
     below = (k + 2 * core + CHIPS - 1) % CHIPS
-    remote(aext.at[pl.ds(4 * other, 5)], gc.at[:, core], halo_send.at[0], halo_recv.at[0], partner)
-    for to in range(2):
-        remote(
-            aext.at[pl.ds(4 * to, 5), edge],
-            rv.at[other],
-            halo_send.at[1 + to],
-            halo_recv.at[1 + other],
-            (2 * below + to, s),
-        )
+    down_here, up_here = k > 0, k < CHIPS - 1
+    vertical = jnp.where(core == 0, down_here, up_here)
     for to in range(2):
         away = right if to == 0 else left
+        within = s < SPACE - 1 if to == 0 else s > 0
         side_slots = slice(8 - 8 * to, 10 - 8 * to)
-        remote(
-            aext.at[side_slots], rh.at[core], halo_send.at[3 + to], halo_recv.at[3 + core], (2 * k + to, away)
-        )
-        remote(
-            aext.at[side_slots, edge],
-            rd.at[other],
-            halo_send.at[5 + to],
-            halo_recv.at[5 + other],
-            (2 * below + to, away),
-        )
+
+        @pl.when(within)
+        def _(to=to, away=away, side_slots=side_slots):
+            remote(
+                aext.at[side_slots],
+                rh.at[core],
+                halo_send.at[3 + to],
+                halo_recv.at[3 + core],
+                (2 * k + to, away),
+            )
+
+        @pl.when(jnp.logical_and(within, vertical))
+        def _(to=to, away=away, side_slots=side_slots):
+            remote(
+                aext.at[side_slots, edge],
+                rd.at[other],
+                halo_send.at[5 + to],
+                halo_recv.at[5 + other],
+                (2 * below + to, away),
+            )
+
+    remote(aext.at[pl.ds(4 * other, 5)], gc.at[:, core], halo_send.at[0], halo_recv.at[0], partner)
+
+    @pl.when(vertical)
+    def _():
+        for to in range(2):
+            remote(
+                aext.at[pl.ds(4 * to, 5), edge],
+                rv.at[other],
+                halo_send.at[1 + to],
+                halo_recv.at[1 + other],
+                (2 * below + to, s),
+            )
+
+    for d in (1, 7):
+        tell(0, over_z(d))
+    for d in (1, 3):
+        tell(1, over_parts(d))
     first_round(mi_ref, mi_all, send.at[1], recv.at[1])
 
     spot = lax.broadcasted_iota(jnp.int32, (32, 128), 1)
@@ -281,26 +314,40 @@
 
     inner, outer = 2 - 2 * core, 3 * core
     wait(gc.at[:, core], halo_recv.at[0])
-    for i in range(2):
-        wait(rv.at[i], halo_recv.at[1 + i])
+    for i, here in ((0, down_here), (1, up_here)):
+
+        @pl.when(here)
+        def _(i=i):
+            wait(rv.at[i], halo_recv.at[1 + i])
+
     mine = stem_of(inner, 3, False)
     spread(mine, mine, send.at[2], recv.at[2])
-    for i in range(2):
-        wait(rh.at[i], halo_recv.at[3 + i])
-        wait(rd.at[i], halo_recv.at[5 + i])
+    beside = jnp.logical_or(at_left, at_right)
+    for i, here in ((0, down_here), (1, up_here)):
+
+        @pl.when(beside)
+        def _(i=i):
+            wait(rh.at[i], halo_recv.at[3 + i])
+
+        @pl.when(jnp.logical_and(beside, here))
+        def _(i=i):
+            wait(rd.at[i], halo_recv.at[5 + i])
+
     mine = stem_of(outer, 2, True)
-    spread(mine, mine, send.at[16], recv.at[16])
-
+    spread(mine, mine, send.at[16], recv.at[16], True)
+
+    pl.semaphore_wait(meet.at[0], 2)
+    pl.semaphore_wait(meet.at[1], 2)
+    for d in (2, 6):
+        tell(2, over_z(d))
     wait(xall.at[:3, :80], recv.at[2])
     forward(functools.partial(x_half, inner, 3), send.at[9], recv.at[9])
-    wait(xall.at[:2, :80], recv.at[16])
-    forward(functools.partial(x_half, outer, 2), send.at[17], recv.at[17])
     wait(mi_all.at[:192], recv.at[1])
     second_round(mi_all, send.at[10], recv.at[10], False)
 
     wait(wall.at[0], recv.at[0])
     wait(xall.at[:3, :32], recv.at[9])
-    wait(xall.at[:2, :32], recv.at[17])
+    wait(xall.at[:2, :112], recv.at[16])
     tokens = xall[...].reshape(640, 512)
     low = lax.broadcasted_iota(jnp.int32, (1, 128), 1) < 64
     bias_row = eb_ref[pl.ds(k, 1), :]
@@ -356,22 +403,20 @@
     for band in range(8):
         hs[band] = summed[16 * band : 16 * band + 16]
 
-    @pl.loop(1, 8)
-    def _(d):
-        to = (z + d) % 8
-        remote(hs.at[to], rs.at[z], send.at[6], recv.at[6], (c, 4 * to + part))
-
-    wait(mo_all.at[:192], recv.at[3])
-    second_round(mo_all, send.at[11], recv.at[11], True)
+    pl.semaphore_wait(meet.at[2], 2)
+    for d in (4, 3, 5, 2, 6, 1, 7):
+        remote(hs.at[(z + d) % 8], rs.at[z], send.at[6], recv.at[6], over_z(d))
+
     rs[z] = hs[z]
     wait(rs.at[:7], recv.at[6])
     total = rs[0].astype(F32)
     for source in range(1, 8):
         total = total + rs[source].astype(F32)
     quarter[part] = total.astype(BF16)
-    for d in range(1, 4):
-        to = 4 * z + (part + d) % 4
-        remote(quarter.at[part], quarter.at[part], send.at[7], recv.at[7], (c, to))
+    for d in (2, 1, 3):
+        remote(quarter.at[part], quarter.at[part], send.at[7], recv.at[7], over_parts(d))
+    wait(mo_all.at[:192], recv.at[3])
+    second_round(mo_all, send.at[11], recv.at[11], True)
     wait(quarter.at[:3], recv.at[7])
     total = quarter[0].astype(F32)
     for source in range(1, 4):
@@ -384,9 +429,8 @@
     total = total + jnp.concatenate(hidden_bias, axis=1)
     act[z] = gelu(total).astype(BF16)
 
-    @pl.loop(1, 8)
-    def _(d):
-        remote(act.at[z], act.at[z], send.at[12], recv.at[12], (c, (s + 4 * d) % SPACE))
+    for d in (4, 3, 5, 2, 6, 1, 7):
+        remote(act.at[z], act.at[z], send.at[12], recv.at[12], over_z(d))
 
     wait(mo_all.at[:192], recv.at[11])
     third_round(mo_all, send.at[14], recv.at[14])
@@ -411,14 +455,25 @@
         out_ref[:, span] = (mine[:, span] + pr[half].astype(F32)).astype(BF16)
 
     wait(gc.at[:, core], halo_send.at[0])
-    for i in range(2):
-        wait(rv.at[i], halo_send.at[1 + i])
-        wait(rh.at[i], halo_send.at[3 + i])
-        wait(rd.at[i], halo_send.at[5 + i])
+    for to in range(2):
+        within = s < SPACE - 1 if to == 0 else s > 0
+
+        @pl.when(vertical)
+        def _(to=to):
+            wait(rv.at[to], halo_send.at[1 + to])
+
+        @pl.when(within)
+        def _(to=to):
+            wait(rh.at[to], halo_send.at[3 + to])
+
+        @pl.when(jnp.logical_and(within, vertical))
+        def _(to=to):
+            wait(rd.at[to], halo_send.at[5 + to])
+
     wait(wall.at[0], send.at[0])
     wait(mi_all.at[:192], send.at[1])
     wait(xall.at[:3, :80], send.at[2])
-    wait(xall.at[:2, :80], send.at[16])
+    wait(xall.at[:2, :112], send.at[16])
     wait(mo_all.at[:192], send.at[3])
     wait(st.at[:15], send.at[4])
     wait(eh.at[0], send.at[5])
@@ -427,7 +482,6 @@
     wait(po.at[0], send.at[8])
     wait(po.at[1], send.at[15])
     wait(xall.at[:3, :32], send.at[9])
-    wait(xall.at[:2, :32], send.at[17])
     wait(mi_all.at[:192], send.at[10])
     wait(mo_all.at[:192], send.at[11])
     wait(mi_all.at[:64], send.at[13])
@@ -486,6 +540,7 @@
             pltpu.SemaphoreType.DMA((18,)),
             pltpu.SemaphoreType.DMA((18,)),
             pltpu.SemaphoreType.DMA((11,)),
+            pltpu.SemaphoreType.REGULAR((3,)),
         ],
         compiler_params=pltpu.CompilerParams(collective_id=0, has_side_effects=True, vmem_limit_bytes=58 * 2**20),
     )(

time: 56.2 us -> 54.2 us (0.964)
  Pallas kernels: 55.4 us -> 53.4 us
    pallas_call x1, Pallas kernels: 55.4 us -> 53.4 us  [shards(): pl.pallas_call(kernel, out_shape=pltpu.VMEM((64, 1024), BF16), in_specs=[...]
where the time goes in v6:
time: 54.2 us; the launch traced here: 54 us
  Pallas kernels  53.4 us (99%)
  local copies, waits for them, and re-layouts  0.66 us (1%)
    pallas_call x1, Pallas kernels, shards(): pl.pallas_call(kernel, out_shape=pltpu.VMEM((64, 1024), BF16), in_specs=[...  53.4 us

profile of v6, /device:TPU:1, one launch (start us, length us, event | category | flops | bytes accessed | tf_op | source)
XLA Modules:
  0.0 54.0 jit_solution(227100499349582957)
XLA Ops:
  0.0 53.4 %shard_map.109 = bf16[64,1024]{1,0:T(8,128)(2,1)S(1)} custom-call(bf16[3,3,20,32]{3,2,1,0:T(8,128)(2,1)} %stem_in.1, f32[1,32]{1,0:T(1,128)} %bitcast.17, f32[8,128]{1,0:T(8,128)} %bitcast.12, f32[8,128]{1,0:T(8,128)} %bitcast.13, f32[8,128]{1,0:T(8,128)} %bitcast.14, f32[8,128]{1,0:T(8,128)} %bitcast.15, f32[1,1024]{1,0:T(1,128)} %bitcast.16, ...), custom_call_target="tpu_custom_call" | custom-call | tf_op jit(solution)/shard_map/pallas_call | solution.py:505
  53.4 0.7 %copy.13 = bf16[1,64,1024]{2,1,0:T(8,128)(2,1)} copy(bf16[1,64,1024]{2,1,0:T(8,128)(2,1)S(1)} %bitcast.9) | data formatting | bytes 262144

commit v7 on v6

--- a/solution.py
+++ b/solution.py
@@ -62,6 +62,12 @@
     halo_recv,
     send,
     recv,
+    rs_send,
+    rs_recv,
+    quarter_send,
+    quarter_recv,
+    act_send,
+    act_recv,
     local,
     meet,
 ):
@@ -147,10 +153,6 @@
     def greet(to):
         pl.semaphore_signal(barrier, inc=1, device_id=to, device_id_type=MESH)
 
-    @pl.loop(1, 16)
-    def _(d):
-        greet(((c + d) % 16, s))
-
     def over_z(d):
         return (c, (s + 4 * d) % SPACE)
 
@@ -163,8 +165,9 @@
         greet(over_parts(d))
     greet((c, side))
     greet((2 * k + other, side))
-    greet(((2 * k + 15) % 16, side))
-    greet(((2 * k + 2) % 16, side))
+    above_us, below_us = ((2 * k + 15) % 16, s), ((2 * k + 2) % 16, s)
+    for to in (above_us, below_us, partner, *near):
+        greet(to)
 
     own_filters = fetch(filters_in, filters, 1)
     own_stem = fetch(stem_in, stem_ref, 2)
@@ -187,7 +190,7 @@
         aext[2 * pair] = window[:, :128]
         aext[2 * pair + 1] = window[:, 128:]
 
-    pl.semaphore_wait(barrier, 23)
+    pl.semaphore_wait(barrier, 14)
 
     def tell(index, to):
         pl.semaphore_signal(meet.at[index], inc=1, device_id=to, device_id_type=MESH)
@@ -210,16 +213,6 @@
                 halo_send.at[3 + to],
                 halo_recv.at[3 + core],
                 (2 * k + to, away),
-            )
-
-        @pl.when(jnp.logical_and(within, vertical))
-        def _(to=to, away=away, side_slots=side_slots):
-            remote(
-                aext.at[side_slots, edge],
-                rd.at[other],
-                halo_send.at[5 + to],
-                halo_recv.at[5 + other],
-                (2 * below + to, away),
             )
 
     remote(aext.at[pl.ds(4 * other, 5)], gc.at[:, core], halo_send.at[0], halo_recv.at[0], partner)
@@ -235,11 +228,32 @@
                 (2 * below + to, s),
             )
 
+    for to in (above_us, below_us):
+        tell(3, to)
     for d in (1, 7):
         tell(0, over_z(d))
     for d in (1, 3):
         tell(1, over_parts(d))
+    for to in (chip(ring, ahead), chip(ring, behind)):
+        tell(4, to)
     first_round(mi_ref, mi_all, send.at[1], recv.at[1])
+
+    pl.semaphore_wait(meet.at[3], 2)
+    for to in range(2):
+        away = right if to == 0 else left
+        within = s < SPACE - 1 if to == 0 else s > 0
+        side_slots = slice(8 - 8 * to, 10 - 8 * to)
+
+        @pl.when(jnp.logical_and(within, vertical))
+        def _(to=to, away=away, side_slots=side_slots):
+            remote(
+                aext.at[side_slots, edge],
+                rd.at[other],
+                halo_send.at[5 + to],
+                halo_recv.at[5 + other],
+                (2 * below + to, away),
+            )
+
 
     spot = lax.broadcasted_iota(jnp.int32, (32, 128), 1)
     repeat = (spot % 32 == lax.broadcasted_iota(jnp.int32, (32, 128), 0)).astype(BF16)
@@ -333,6 +347,7 @@
         def _(i=i):
             wait(rd.at[i], halo_recv.at[5 + i])
 
+    pl.semaphore_wait(meet.at[4], 2)
     mine = stem_of(outer, 2, True)
     spread(mine, mine, send.at[16], recv.at[16], True)
 
@@ -369,9 +384,11 @@
         for kind in range(2):
             st[c, kind : kind + 1, 128 * column : 128 * column + 128] = sums[column][kind]
 
-    @pl.loop(1, 16)
-    def _(d):
-        remote(st.at[c], st.at[c], send.at[4], recv.at[4], ((c + d) % 16, s))
+    for r, step in ((1, 2), (0, 2), (1, 1), (1, 3), (0, 1), (0, 3), (1, 0), (0, 0)):
+        for which in (other, core):
+            if r or step or which is other:
+                to = 2 * (4 * (1 - ring if r else ring) + (x + step) % 4) + which
+                remote(st.at[c], st.at[c], send.at[4], recv.at[4], (to, s))
 
     remote(eh.at[core], eh.at[core], send.at[5], recv.at[5], partner)
 
@@ -398,55 +415,66 @@
 
     own_mi.wait()
     wait(mi_all.at[:64], recv.at[13])
-    summed = lax.dot_general(normed, mi_all[...], (((1,), (1,)), ((), ())), preferred_element_type=F32)
-    summed = summed.astype(BF16)
-    for band in range(8):
-        hs[band] = summed[16 * band : 16 * band + 16]
-
     pl.semaphore_wait(meet.at[2], 2)
-    for d in (4, 3, 5, 2, 6, 1, 7):
-        remote(hs.at[(z + d) % 8], rs.at[z], send.at[6], recv.at[6], over_z(d))
-
-    rs[z] = hs[z]
-    wait(rs.at[:7], recv.at[6])
-    total = rs[0].astype(F32)
-    for source in range(1, 8):
-        total = total + rs[source].astype(F32)
-    quarter[part] = total.astype(BF16)
-    for d in (2, 1, 3):
-        remote(quarter.at[part], quarter.at[part], send.at[7], recv.at[7], over_parts(d))
-    wait(mo_all.at[:192], recv.at[3])
-    second_round(mo_all, send.at[11], recv.at[11], True)
-    wait(quarter.at[:3], recv.at[7])
-    total = quarter[0].astype(F32)
-    for source in range(1, 4):
-        total = total + quarter[source].astype(F32)
+    for half in range(2):
+        units = slice(256 * half, 256 * half + 256)
+        summed = lax.dot_general(normed, mi_all[units], (((1,), (1,)), ((), ())), preferred_element_type=F32)
+        summed = summed.astype(BF16)
+        for band in range(8):
+            hs[half, band] = summed[16 * band : 16 * band + 16]
+        for d in (4, 3, 5, 2, 6, 1, 7):
+            remote(hs.at[half, (z + d) % 8], rs.at[half, z], rs_send.at[half], rs_recv.at[half], over_z(d))
+
+    for half in range(2):
+        rs[half, z] = hs[half, z]
+        wait(rs.at[half, :7], rs_recv.at[half])
+        total = rs[half, 0].astype(F32)
+        for source in range(1, 8):
+            total = total + rs[half, source].astype(F32)
+        quarter[half, part] = total.astype(BF16)
+        mine = quarter.at[half, part]
+        for d in (2, 1, 3):
+            remote(mine, mine, quarter_send.at[half], quarter_recv.at[half], over_parts(d))
+        if half == 0:
+            wait(mo_all.at[:192], recv.at[3])
+            second_round(mo_all, send.at[11], recv.at[11], True)
     rows = mb_ref[...]
     turned = pltpu.roll(rows, 64, axis=1)
     ours = jnp.where(low, jnp.where(core == 0, rows, turned), 0.0)
     theirs = jnp.where(low, 0.0, jnp.where(core == 0, turned, rows))
     hidden_bias = [ours[2 * i : 2 * i + 1] + theirs[2 * i + 1 : 2 * i + 2] for i in range(4)]
-    total = total + jnp.concatenate(hidden_bias, axis=1)
-    act[z] = gelu(total).astype(BF16)
-
-    for d in (4, 3, 5, 2, 6, 1, 7):
-        remote(act.at[z], act.at[z], send.at[12], recv.at[12], over_z(d))
+    for half in range(2):
+        wait(quarter.at[half, :3], quarter_recv.at[half])
+        total = quarter[half, 0].astype(F32)
+        for source in range(1, 4):
+            total = total + quarter[half, source].astype(F32)
+        total = total + jnp.concatenate(hidden_bias[2 * half : 2 * half + 2], axis=1)
+        act[half, z] = gelu(total).astype(BF16)
+        for d in (4, 3, 5, 2, 6, 1, 7):
+            remote(act.at[half, z], act.at[half, z], act_send.at[half], act_recv.at[half], over_z(d))
 
     wait(mo_all.at[:192], recv.at[11])
     third_round(mo_all, send.at[14], recv.at[14])
     own_mo.wait()
-    wait(act.at[:7], recv.at[12])
+
+    def rows_of(which, half):
+        return act[half, pl.ds(4 * which, 4)].reshape(64, 256)
+
+    def product(which, half):
+        units = slice(256 * half, 256 * half + 256)
+        return jnp.dot(rows_of(which, half), mo_all[units], preferred_element_type=F32)
+
+    wait(act.at[0, :7], act_recv.at[0])
     wait(mo_all.at[:64], recv.at[14])
-
-    def rows_of(which):
-        return act[pl.ds(4 * which, 4)].reshape(64, 512)
-
-    others = rows_of(other)
-    for half in range(2):
-        part_out = jnp.dot(others, mo_all[:, 512 * half : 512 * half + 512], preferred_element_type=F32)
-        po[half] = part_out.astype(BF16)
+    early = product(other, 0)
+    mine = product(core, 0) + ob_ref[...]
+    wait(act.at[1, :7], act_recv.at[1])
+    for half in range(2):
+        span = slice(512 * half, 512 * half + 512)
+        late = jnp.dot(rows_of(other, 1), mo_all[256:512, span], preferred_element_type=F32)
+        po[half] = (early[:, span] + late).astype(BF16)
         remote(po.at[half], pr.at[half], send.at[8 + 7 * half], recv.at[8 + 7 * half], partner)
-    mine = jnp.dot(rows_of(core), mo_all[...], preferred_element_type=F32) + ob_ref[...]
+    mine = mine + product(core, 1)
     residual = [eh[half, pl.ds(pl.multiple_of(64 * core, 64), 64), :].astype(F32) for half in range(2)]
     mine = mine + jnp.concatenate(residual, axis=1)
     for half in range(2):
@@ -477,8 +505,10 @@
     wait(mo_all.at[:192], send.at[3])
     wait(st.at[:15], send.at[4])
     wait(eh.at[0], send.at[5])
-    wait(rs.at[:7], send.at[6])
-    wait(quarter.at[:3], send.at[7])
+    for half in range(2):
+        wait(rs.at[half, :7], rs_send.at[half])
+        wait(quarter.at[half, :3], quarter_send.at[half])
+        wait(act.at[half, :7], act_send.at[half])
     wait(po.at[0], send.at[8])
     wait(po.at[1], send.at[15])
     wait(xall.at[:3, :32], send.at[9])
@@ -486,7 +516,6 @@
     wait(mo_all.at[:192], send.at[11])
     wait(mi_all.at[:64], send.at[13])
     wait(mo_all.at[:64], send.at[14])
-    wait(act.at[:7], send.at[12])
 
 
 def shards(
@@ -529,18 +558,19 @@
             pltpu.VMEM((16, 2, 512), F32),
             pltpu.VMEM((512, 1024), BF16),
             pltpu.VMEM((512, 1024), BF16),
-            pltpu.VMEM((8, 16, 512), BF16),
-            pltpu.VMEM((8, 16, 512), BF16),
-            pltpu.VMEM((4, 16, 512), BF16),
-            pltpu.VMEM((8, 16, 512), BF16),
+            pltpu.VMEM((2, 8, 16, 256), BF16),
+            pltpu.VMEM((2, 8, 16, 256), BF16),
+            pltpu.VMEM((2, 4, 16, 256), BF16),
+            pltpu.VMEM((2, 8, 16, 256), BF16),
             pltpu.VMEM((2, 64, 512), BF16),
             pltpu.VMEM((2, 64, 512), BF16),
             pltpu.SemaphoreType.DMA((7,)),
             pltpu.SemaphoreType.DMA((7,)),
             pltpu.SemaphoreType.DMA((18,)),
             pltpu.SemaphoreType.DMA((18,)),
+            *[pltpu.SemaphoreType.DMA((2,))] * 6,
             pltpu.SemaphoreType.DMA((11,)),
-            pltpu.SemaphoreType.REGULAR((3,)),
+            pltpu.SemaphoreType.REGULAR((5,)),
         ],
         compiler_params=pltpu.CompilerParams(collective_id=0, has_side_effects=True, vmem_limit_bytes=58 * 2**20),
     )(

time: 54.2 us -> 52.5 us (0.969)
  Pallas kernels: 53.4 us -> 51.7 us
    pallas_call x1, Pallas kernels: 53.4 us -> 51.7 us  [shards(): pl.pallas_call(kernel, out_shape=pltpu.VMEM((64, 1024), BF16), in_specs=[...]
where the time goes in v7:
time: 52.5 us; the launch traced here: 52.4 us
  Pallas kernels  51.7 us (98%)
  local copies, waits for them, and re-layouts  0.66 us (1%)
    pallas_call x1, Pallas kernels, shards(): pl.pallas_call(kernel, out_shape=pltpu.VMEM((64, 1024), BF16), in_specs=[...  51.7 us

profile of v7, /device:TPU:1, one launch (start us, length us, event | category | flops | bytes accessed | tf_op | source)
XLA Modules:
  0.0 52.4 jit_solution(1820706949130522594)
XLA Ops:
  0.0 51.7 %shard_map.109 = bf16[64,1024]{1,0:T(8,128)(2,1)S(1)} custom-call(bf16[3,3,20,32]{3,2,1,0:T(8,128)(2,1)} %stem_in.1, f32[1,32]{1,0:T(1,128)} %bitcast.17, f32[8,128]{1,0:T(8,128)} %bitcast.12, f32[8,128]{1,0:T(8,128)} %bitcast.13, f32[8,128]{1,0:T(8,128)} %bitcast.14, f32[8,128]{1,0:T(8,128)} %bitcast.15, f32[1,1024]{1,0:T(1,128)} %bitcast.16, ...), custom_call_target="tpu_custom_call" | custom-call | tf_op jit(solution)/shard_map/pallas_call | solution.py:534
  51.7 0.7 %copy.13 = bf16[1,64,1024]{2,1,0:T(8,128)(2,1)} copy(bf16[1,64,1024]{2,1,0:T(8,128)(2,1)S(1)} %bitcast.9) | data formatting | bytes 262144

commit v8 on v7

--- a/solution.py
+++ b/solution.py
@@ -98,16 +98,15 @@
 
     far = [chip(1 - ring, (x + 2) % 4), chip(ring, (x + 2) % 4)]
 
-    def spread(src, dst, ssem, rsem, everyone=False):
-        for to in far + near[::-1] if everyone else near:
+    def spread(src, dst, ssem, rsem):
+        for to in far + near[::-1]:
             remote(src, dst, ssem, rsem, to)
 
-    def forward(half, ssem, rsem):
-        for r in range(2):
-            passed = half(4 * r + behind, 0)
-            remote(passed, passed, ssem, rsem, chip(ring, ahead))
-            passed = half(4 * r + ahead, 1)
-            remote(passed, passed, ssem, rsem, chip(ring, behind))
+    def forward(half, r, ssem, rsem):
+        passed = half(4 * r + behind, 0)
+        remote(passed, passed, ssem, rsem, chip(ring, ahead))
+        passed = half(4 * r + ahead, 1)
+        remote(passed, passed, ssem, rsem, chip(ring, behind))
 
     def rows_from(buffer, owner, start, size):
         return buffer.at[pl.ds(pl.multiple_of(64 * owner + start, 16), size)]
@@ -159,12 +158,27 @@
     def over_parts(d):
         return (c, 4 * z + (part + d) % 4)
 
-    for d in (1, 7):
-        greet(over_z(d))
+    def line_z(d, act_on):
+        @pl.when(z >= d)
+        def _():
+            act_on((c, s - 4 * d))
+
+        @pl.when(z + d < 8)
+        def _():
+            act_on((c, s + 4 * d))
+
+    def on_line(d):
+        return (z >= d).astype(jnp.int32) + (z + d < 8).astype(jnp.int32)
+
+    line_z(1, greet)
     for d in (1, 3):
         greet(over_parts(d))
-    greet((c, side))
-    greet((2 * k + other, side))
+
+    @pl.when(jnp.where(core == 0, s > 0, s < SPACE - 1))
+    def _():
+        greet((c, side))
+        greet((2 * k + other, side))
+
     above_us, below_us = ((2 * k + 15) % 16, s), ((2 * k + 2) % 16, s)
     for to in (above_us, below_us, partner, *near):
         greet(to)
@@ -190,7 +204,8 @@
         aext[2 * pair] = window[:, :128]
         aext[2 * pair + 1] = window[:, 128:]
 
-    pl.semaphore_wait(barrier, 14)
+    beside_us = (s > 0).astype(jnp.int32) + (s < SPACE - 1).astype(jnp.int32)
+    pl.semaphore_wait(barrier, 10 + on_line(1) + beside_us)
 
     def tell(index, to):
         pl.semaphore_signal(meet.at[index], inc=1, device_id=to, device_id_type=MESH)
@@ -230,8 +245,7 @@
 
     for to in (above_us, below_us):
         tell(3, to)
-    for d in (1, 7):
-        tell(0, over_z(d))
+    line_z(1, functools.partial(tell, 0))
     for d in (1, 3):
         tell(1, over_parts(d))
     for to in (chip(ring, ahead), chip(ring, behind)):
@@ -335,7 +349,9 @@
             wait(rv.at[i], halo_recv.at[1 + i])
 
     mine = stem_of(inner, 3, False)
-    spread(mine, mine, send.at[2], recv.at[2])
+    for i, to in enumerate(near):
+        remote(mine, mine, send.at[2], recv.at[2 if i < 2 else 12], to)
+
     beside = jnp.logical_or(at_left, at_right)
     for i, here in ((0, down_here), (1, up_here)):
 
@@ -349,14 +365,17 @@
 
     pl.semaphore_wait(meet.at[4], 2)
     mine = stem_of(outer, 2, True)
-    spread(mine, mine, send.at[16], recv.at[16], True)
-
-    pl.semaphore_wait(meet.at[0], 2)
+    spread(mine, mine, send.at[16], recv.at[16])
+
+    pl.semaphore_wait(meet.at[0], on_line(1))
     pl.semaphore_wait(meet.at[1], 2)
-    for d in (2, 6):
-        tell(2, over_z(d))
-    wait(xall.at[:3, :80], recv.at[2])
-    forward(functools.partial(x_half, inner, 3), send.at[9], recv.at[9])
+    line_z(2, functools.partial(tell, 2))
+    wait(xall.at[:3, :32], recv.at[2])
+    forward(functools.partial(x_half, inner, 3), ring, send.at[9], recv.at[9])
+    wait(xall.at[:3, :48], recv.at[12])
+    forward(functools.partial(x_half, inner, 3), 1 - ring, send.at[9], recv.at[9])
+    pl.semaphore_wait(meet.at[2], on_line(2))
+    line_z(4, functools.partial(tell, 5))
     wait(mi_all.at[:192], recv.at[1])
     second_round(mi_all, send.at[10], recv.at[10], False)
 
@@ -415,7 +434,7 @@
 
     own_mi.wait()
     wait(mi_all.at[:64], recv.at[13])
-    pl.semaphore_wait(meet.at[2], 2)
+    pl.semaphore_wait(meet.at[5], 1)
     for half in range(2):
         units = slice(256 * half, 256 * half + 256)
         summed = lax.dot_general(normed, mi_all[units], (((1,), (1,)), ((), ())), preferred_element_type=F32)
@@ -570,7 +589,7 @@
             pltpu.SemaphoreType.DMA((18,)),
             *[pltpu.SemaphoreType.DMA((2,))] * 6,
             pltpu.SemaphoreType.DMA((11,)),
-            pltpu.SemaphoreType.REGULAR((5,)),
+            pltpu.SemaphoreType.REGULAR((6,)),
         ],
         compiler_params=pltpu.CompilerParams(collective_id=0, has_side_effects=True, vmem_limit_bytes=58 * 2**20),
     )(

time: 52.5 us -> 52.4 us (level)
  no operation moved by 1% of the time
where the time goes in v8:
time: 52.4 us; the launch traced here: 52.3 us
  Pallas kernels  51.6 us (98%)
  local copies, waits for them, and re-layouts  0.66 us (1%)
    pallas_call x1, Pallas kernels, shards(): pl.pallas_call(kernel, out_shape=pltpu.VMEM((64, 1024), BF16), in_specs=[...  51.6 us

profile of v8, /device:TPU:1, one launch (start us, length us, event | category | flops | bytes accessed | tf_op | source)
XLA Modules:
  0.0 52.3 jit_solution(11058767876305307743)
XLA Ops:
  0.0 51.6 %shard_map.109 = bf16[64,1024]{1,0:T(8,128)(2,1)S(1)} custom-call(bf16[3,3,20,32]{3,2,1,0:T(8,128)(2,1)} %stem_in.1, f32[1,32]{1,0:T(1,128)} %bitcast.17, f32[8,128]{1,0:T(8,128)} %bitcast.12, f32[8,128]{1,0:T(8,128)} %bitcast.13, f32[8,128]{1,0:T(8,128)} %bitcast.14, f32[8,128]{1,0:T(8,128)} %bitcast.15, f32[1,1024]{1,0:T(1,128)} %bitcast.16, ...), custom_call_target="tpu_custom_call" | custom-call | tf_op jit(solution)/shard_map/pallas_call | solution.py:553
  51.6 0.7 %copy.13 = bf16[1,64,1024]{2,1,0:T(8,128)(2,1)} copy(bf16[1,64,1024]{2,1,0:T(8,128)(2,1)S(1)} %bitcast.9) | data formatting | bytes 262144

commit v9 on v8

--- a/solution.py
+++ b/solution.py
@@ -433,10 +433,12 @@
     normed = jnp.concatenate(normed, axis=1)
 
     own_mi.wait()
-    wait(mi_all.at[:64], recv.at[13])
     pl.semaphore_wait(meet.at[5], 1)
-    for half in range(2):
-        units = slice(256 * half, 256 * half + 256)
+    halves = (ring, 1 - ring)
+    for half in halves:
+        if half is not ring:
+            wait(mi_all.at[:64], recv.at[13])
+        units = pl.ds(pl.multiple_of(256 * half, 256), 256)
         summed = lax.dot_general(normed, mi_all[units], (((1,), (1,)), ((), ())), preferred_element_type=F32)
         summed = summed.astype(BF16)
         for band in range(8):
@@ -444,7 +446,7 @@
         for d in (4, 3, 5, 2, 6, 1, 7):
             remote(hs.at[half, (z + d) % 8], rs.at[half, z], rs_send.at[half], rs_recv.at[half], over_z(d))
 
-    for half in range(2):
+    for half in halves:
         rs[half, z] = hs[half, z]
         wait(rs.at[half, :7], rs_recv.at[half])
         total = rs[half, 0].astype(F32)
@@ -454,7 +456,7 @@
         mine = quarter.at[half, part]
         for d in (2, 1, 3):
             remote(mine, mine, quarter_send.at[half], quarter_recv.at[half], over_parts(d))
-        if half == 0:
+        if half is ring:
             wait(mo_all.at[:192], recv.at[3])
             second_round(mo_all, send.at[11], recv.at[11], True)
     rows = mb_ref[...]
@@ -462,12 +464,13 @@
     ours = jnp.where(low, jnp.where(core == 0, rows, turned), 0.0)
     theirs = jnp.where(low, 0.0, jnp.where(core == 0, turned, rows))
     hidden_bias = [ours[2 * i : 2 * i + 1] + theirs[2 * i + 1 : 2 * i + 2] for i in range(4)]
-    for half in range(2):
+    biases = [jnp.concatenate(hidden_bias[2 * i : 2 * i + 2], axis=1) for i in range(2)]
+    for half in halves:
         wait(quarter.at[half, :3], quarter_recv.at[half])
         total = quarter[half, 0].astype(F32)
         for source in range(1, 4):
             total = total + quarter[half, source].astype(F32)
-        total = total + jnp.concatenate(hidden_bias[2 * half : 2 * half + 2], axis=1)
+        total = total + jnp.where(half == 0, biases[0], biases[1])
         act[half, z] = gelu(total).astype(BF16)
         for d in (4, 3, 5, 2, 6, 1, 7):
             remote(act.at[half, z], act.at[half, z], act_send.at[half], act_recv.at[half], over_z(d))
@@ -480,20 +483,21 @@
         return act[half, pl.ds(4 * which, 4)].reshape(64, 256)
 
     def product(which, half):
-        units = slice(256 * half, 256 * half + 256)
+        units = pl.ds(pl.multiple_of(256 * half, 256), 256)
         return jnp.dot(rows_of(which, half), mo_all[units], preferred_element_type=F32)
 
-    wait(act.at[0, :7], act_recv.at[0])
+    wait(act.at[ring, :7], act_recv.at[ring])
+    early = product(other, ring)
+    mine = product(core, ring) + ob_ref[...]
     wait(mo_all.at[:64], recv.at[14])
-    early = product(other, 0)
-    mine = product(core, 0) + ob_ref[...]
-    wait(act.at[1, :7], act_recv.at[1])
+    wait(act.at[1 - ring, :7], act_recv.at[1 - ring])
+    last = pl.ds(pl.multiple_of(256 * (1 - ring), 256), 256)
     for half in range(2):
         span = slice(512 * half, 512 * half + 512)
-        late = jnp.dot(rows_of(other, 1), mo_all[256:512, span], preferred_element_type=F32)
+        late = jnp.dot(rows_of(other, 1 - ring), mo_all[last, span], preferred_element_type=F32)
         po[half] = (early[:, span] + late).astype(BF16)
         remote(po.at[half], pr.at[half], send.at[8 + 7 * half], recv.at[8 + 7 * half], partner)
-    mine = mine + product(core, 1)
+    mine = mine + product(core, 1 - ring)
     residual = [eh[half, pl.ds(pl.multiple_of(64 * core, 64), 64), :].astype(F32) for half in range(2)]
     mine = mine + jnp.concatenate(residual, axis=1)
     for half in range(2):

time: 52.4 us -> 51.9 us (level)
  no operation moved by 1% of the time
where the time goes in v9:
time: 51.9 us; the launch traced here: 51.8 us
  Pallas kernels  51.1 us (98%)
  local copies, waits for them, and re-layouts  0.66 us (1%)
    pallas_call x1, Pallas kernels, shards(): pl.pallas_call(kernel, out_shape=pltpu.VMEM((64, 1024), BF16), in_specs=[...  51.1 us

profile of v9, /device:TPU:1, one launch (start us, length us, event | category | flops | bytes accessed | tf_op | source)
XLA Modules:
  0.0 51.8 jit_solution(17816140986024496293)
XLA Ops:
  0.0 51.1 %shard_map.109 = bf16[64,1024]{1,0:T(8,128)(2,1)S(1)} custom-call(bf16[3,3,20,32]{3,2,1,0:T(8,128)(2,1)} %stem_in.1, f32[1,32]{1,0:T(1,128)} %bitcast.17, f32[8,128]{1,0:T(8,128)} %bitcast.12, f32[8,128]{1,0:T(8,128)} %bitcast.13, f32[8,128]{1,0:T(8,128)} %bitcast.14, f32[8,128]{1,0:T(8,128)} %bitcast.15, f32[1,1024]{1,0:T(1,128)} %bitcast.16, ...), custom_call_target="tpu_custom_call" | custom-call | tf_op jit(solution)/shard_map/pallas_call | solution.py:557
  51.1 0.7 %copy.13 = bf16[1,64,1024]{2,1,0:T(8,128)(2,1)} copy(bf16[1,64,1024]{2,1,0:T(8,128)(2,1)S(1)} %bitcast.9) | data formatting | bytes 262144
